TPU v7x, 512 devices: a whole 4x8x8 slice. The times are simulated.
512 devices in a mesh: load: 8 (over y_hi, core), brick: 64 (over z, y_lo, x).
Axes of the slice: x: 4, y: 8 (y_hi: 4, y_lo: 2; y = y_hi * 2 + y_lo), z: 8, core: 2. Of those that a mesh axis runs over, the one named last changes fastest.
Arguments:
- density: float32 [768, 64, 128], P('brick'), may hold values from 0.1 to 0.95
- passive: int32 [768, 64, 128], P('brick'), may hold values from 0 to 2, as said below
- support: int32 [768, 64, 128], P('brick'), may hold values 0 or 1
- load_nodes: int32 [16, 64], P('load'), may hold values from 0 to 6291455
- load_force: float32 [16, 64], P('load'), may hold values from -6 to 6
- self_weight: float32 [16], P('load'), may hold values from 0.3 to 3
- body_force: float32 [16, 768, 64, 128], P('load', 'brick'), may hold values from -3 to 3
Outputs:
- new_density: float32 [768, 64, 128], P('brick', 'load')
- momentum: float32 [768, 64, 128], P('brick', 'load')
- displacement: float32 [16, 768, 64, 128], P('load', 'brick')
Inputs may be any that keep to these rules, and one draw needn't show every extreme that they name: 0 marks a design voxel, 1 a passive void voxel, 2 a passive solid voxel.
All inputs are finite; a program needn't handle non-finite values. No bound on the sum of `support` on one device may be relied on, other than what follows from the above.
Results may differ from a plain program's by a relative error of at most 0.0001.
Values sent between devices are 32-bit elements; how exact they have to be, the bound alone decides.
A program may use at most 64 MiB of HBM per device.

v0:
```python
import jax
import jax.numpy as jnp
from jax import lax
from jax.sharding import PartitionSpec as P

SWEEPS = 5
DESIGN_ITERS = 2


stiff_floor = 0.01
mass_shift = 0.1
spectrum_low = 0.05
spectrum_high = 2.0
moment_decay = 0.8
step_size = 0.1
volume_pull = 0.5
volume_target = 0.4
density_floor = 0.001


def padded_2(block, sides, width):
    for axis, dim in sides:
        count = lax.axis_size(axis)
        forward = [(i, i + 1) for i in range(count - 1)]
        backward = [(target, source) for source, target in forward]
        low = lax.ppermute(
            lax.slice_in_dim(block, block.shape[dim] - width, None, axis=dim), axis, forward
        )
        high = lax.ppermute(lax.slice_in_dim(block, 0, width, axis=dim), axis, backward)
        block = jnp.concatenate([low, block, high], axis=dim)
    return block


def neighbours(padded):
    return (
        padded[..., 2:, 1:-1, 1:-1],
        padded[..., :-2, 1:-1, 1:-1],
        padded[..., 1:-1, 2:, 1:-1],
        padded[..., 1:-1, :-2, 1:-1],
        padded[..., 1:-1, 1:-1, 2:],
        padded[..., 1:-1, 1:-1, :-2],
    )


def pad_sides(vector, leading):
    return jnp.pad(vector, ((0, 0),) * (leading + 1) + ((1, 1), (1, 1)))


def brick_pad(vector):
    return pad_sides(padded_2(vector, (("brick", 1),), 1), 1)


def passive_apply(design, passive):
    return jnp.where(passive == 1, density_floor, jnp.where(passive == 2, 1.0, design))


def operate(vector, free_mask, stiffness, face_list, padded_free):
    freed = padded_free[..., 1:-1, 1:-1, 1:-1]
    accumulated = mass_shift * stiffness * freed
    for face_weight, beside in zip(face_list, neighbours(padded_free)):
        accumulated = accumulated + face_weight * (freed - beside)
    return free_mask * accumulated + (1.0 - free_mask) * vector


def chebyshev(source, free_mask, stiffness, face_list, diagonal, pad_fn):
    centre = 0.5 * (spectrum_high + spectrum_low)
    half_width = 0.5 * (spectrum_high - spectrum_low)
    ratio_one = centre / half_width
    previous = 1.0 / ratio_one
    solution = jnp.zeros_like(source)
    residual = source
    direction = residual / diagonal / centre
    for sweep_index in range(SWEEPS):
        solution = solution + direction
        if sweep_index < SWEEPS - 1:
            applied = operate(
                direction, free_mask, stiffness, face_list, pad_fn(free_mask * direction)
            )
            residual = residual - applied
            current = 1.0 / (2.0 * ratio_one - previous)
            direction = current * previous * direction + 2.0 * current / half_width * (
                residual / diagonal
            )
            previous = current
    return solution


def load_energy(freed, padded):
    energy = mass_shift * freed * freed
    for beside in neighbours(padded):
        energy = energy + 0.25 * (freed - beside) ** 2
    return energy


def inside_count(start_x, start_y, grid_shape, total_shape):
    along_x = start_x + lax.broadcasted_iota(jnp.int32, grid_shape, 0)
    along_y = start_y + lax.broadcasted_iota(jnp.int32, grid_shape, 1)
    along_z = lax.broadcasted_iota(jnp.int32, grid_shape, 2)
    edges = (
        (along_x == 0).astype(jnp.float32)
        + (along_x == total_shape[0] - 1).astype(jnp.float32)
        + (along_y == 0).astype(jnp.float32)
        + (along_y == total_shape[1] - 1).astype(jnp.float32)
        + (along_z == 0).astype(jnp.float32)
        + (along_z == total_shape[2] - 1).astype(jnp.float32)
    )
    return 6.0 - edges


def filter_field(sensitivity, padded, neighbour_count):
    accumulated = 2.0 * sensitivity
    for beside in neighbours(padded):
        accumulated = accumulated + beside
    return accumulated / (2.0 + neighbour_count)


def design_step(design, momentum, passive, abs_total, density_total, total_cells):
    mean_step = abs_total / total_cells + 1e-06
    mean_density = density_total / total_cells
    moved = design - step_size * momentum / mean_step - volume_pull * (mean_density - volume_target)
    return passive_apply(jnp.clip(moved, density_floor, 1.0), passive)


def place_points(load_nodes, load_force, first_x, rows_x, size_y, size_z):
    loads_here = load_nodes.shape[0]
    span_cells = rows_x * size_y * size_z
    local_ids = load_nodes - first_x * size_y * size_z
    inside = (local_ids >= 0) & (local_ids < span_cells)
    slot_ids = jnp.where(inside, local_ids, span_cells)
    row_ids = lax.broadcasted_iota(jnp.int32, load_nodes.shape, 0)
    points = (
        jnp.zeros((loads_here, span_cells + 1), jnp.float32).at[row_ids, slot_ids].add(load_force)
    )
    return points[:, :span_cells].reshape(loads_here, rows_x, size_y, size_z)


def face_terms(stiffness, padded, free_mask):
    face_list = tuple((0.5 * (stiffness + beside) for beside in neighbours(padded)))
    face_total = face_list[0]
    for face_weight in face_list[1:]:
        face_total = face_total + face_weight
    diagonal = free_mask * (face_total + mass_shift * stiffness) + (1.0 - free_mask)
    return (face_list, diagonal)


def body(density, passive, support, load_nodes, load_force, self_weight, body_force):
    cells_x, size_y, size_z = density.shape
    brick_count = lax.axis_size("brick")
    brick_index = lax.axis_index("brick")
    load_count = lax.axis_size("load")
    load_index = lax.axis_index("load")
    slab_rows = size_y // load_count
    slab_start = load_index * slab_rows
    total_cells = cells_x * brick_count * size_y * size_z
    free_mask = (1 - support).astype(jnp.float32)
    design = passive_apply(density, passive)
    points = place_points(load_nodes, load_force, brick_index * cells_x, cells_x, size_y, size_z)
    design_here = design
    start_y = 0
    momentum = jnp.zeros_like(design_here)
    neighbour_count = inside_count(
        brick_index * cells_x, start_y, design_here.shape, (cells_x * brick_count, size_y, size_z)
    )
    displacement = None
    for iteration in range(DESIGN_ITERS):
        stiffness = stiff_floor + (1.0 - stiff_floor) * design**3
        stiff_padded = pad_sides(padded_2(stiffness, (("brick", 0),), 1), 0)
        face_list, diagonal = face_terms(stiffness, stiff_padded, free_mask)
        source = free_mask * (points + self_weight[:, None, None, None] * design + body_force)
        displacement = chebyshev(source, free_mask, stiffness, face_list, diagonal, brick_pad)
        freed = free_mask * displacement
        local_energy = jnp.sum(load_energy(freed, brick_pad(freed)), axis=0)
        energy = lax.psum(local_energy, "load")
        sensitivity = -3.0 * (1.0 - stiff_floor) * design_here * design_here * energy
        padded = pad_sides(padded_2(sensitivity, (("brick", 0),), 1), 0)
        filtered = filter_field(sensitivity, padded, neighbour_count)
        momentum = moment_decay * momentum + filtered
        abs_total, density_total = lax.psum(
            (jnp.sum(jnp.abs(momentum)), jnp.sum(design_here)), "brick"
        )
        design_here = design_step(
            design_here, momentum, passive, abs_total, density_total, total_cells
        )
        design = design_here
    return (
        lax.dynamic_slice_in_dim(design_here, slab_start, slab_rows, 1),
        lax.dynamic_slice_in_dim(momentum, slab_start, slab_rows, 1),
        displacement,
    )


def solution(mesh):
    placed = (
        P("brick", None, None),
        P("brick", None, None),
        P("brick", None, None),
        P("load", None),
        P("load", None),
        P("load"),
        P("load", "brick", None, None),
    )
    return jax.shard_map(
        body,
        mesh=mesh,
        in_specs=placed,
        out_specs=(
            P("brick", "load", None),
            P("brick", "load", None),
            P("load", "brick", None, None),
        ),
        check_vma=False,
    )
```

profile of v0, /device:TPU:258, one launch (start us, length us, event | category | flops | bytes accessed | tf_op | source)
XLA Modules:
  0.0 702.6 jit_solution(10898506315707322790)
XLA Ops:
  7.2 2.6 fusion.233
  9.9 2.4 collective-permute-start
  12.4 3.4 collective-permute-start.1
  16.2 7.0 scatter_fusion
  25.0 1.5 multiply_add_fusion.7
  27.2 3.3 collective-permute-start.2
  30.5 2.5 collective-permute-start.3
  33.4 7.5 %collective-permute-done.3 = f32[2,1,64,128]{3,2,1,0:T(8,128)S(1)} collective-permute-done((f32[2,1,64,128]{3,2,1,0:T(8,128)S(1)}, f32[2,1,64,128]{3,2,1,0:T(8,128)S(1)}, u32[]{:S(2)}, u32[]{:S(2)}) %collective-permute-start.3) | collective-permute-done | bytes 65568 | tf_op jit(solution)/shard_map/ppermute | solution.py:26
  41.5 1.3 broadcast_multiply_fusion.6
  42.9 8.1 %collective-permute-start.4 = (f32[2,1,64,128]{3,2,1,0:T(8,128)S(1)}, f32[2,1,64,128]{3,2,1,0:T(8,128)S(1)}, u32[]{:S(2)}, u32[]{:S(2)}) collective-permute-start(f32[2,1,64,128]{3,2,1,0:T(8,128)S(1)} %get-tuple-element.68), channel_id=1, source_target_pairs={{1,0},{2,1},{3,2},{4,3},{5,4},{6,5},{7,6},{8,7},{9,8},{10,9},{11,1... | collective-permute-start | bytes 196616 | tf_op jit(solution)/shard_map/ppermute | solution.py:29
  51.0 1.9 collective-permute-start.5
  53.0 4.2 collective-permute-done.5
  57.8 1.2 broadcast_multiply_fusion.5
  59.0 6.1 collective-permute-start.6
  65.2 1.9 collective-permute-start.7
  67.1 4.2 collective-permute-done.7
  71.9 1.1 fusion.186
  73.1 6.1 collective-permute-start.8
  79.2 1.9 collective-permute-start.9
  81.2 4.2 collective-permute-done.9
  86.0 1.7 add_multiply_fusion.1
  87.8 6.1 collective-permute-start.10
  93.9 2.1 collective-permute-start.11
  96.0 4.0 collective-permute-done.11
  100.7 1.8 fusion.12
  102.6 81.1 %all-reduce.19.cloned.1.call-done = f32[12,64,128]{2,1,0:T(8,128)} async-done(((f32[12,64,128]{2,1,0:T(8,128)}), f32[12,64,128]{2,1,0:T(8,128)}) %all-reduce.19.cloned.1.call-update) | async-done | bytes 393232 | tf_op jit(solution)/shard_map/psum | solution.py:173
  183.6 1.0 fusion.188
  184.7 2.5 collective-permute-start.12
  187.2 3.4 collective-permute-start.13
  190.6 3.0 collective-permute-done.13
  193.9 1.8 abs_reduce_fusion.1
  195.7 159.2 %all-reduce.15 = (f32[]{:T(128)}, f32[]{:T(128)}) all-reduce(f32[]{:T(128)} %get-tuple-element.27, f32[]{:T(128)} %get-tuple-element.25), channel_id=1, replica_groups=mesh['load'=8,'brick'=64] {'brick'}, use_global_device_ids=true, to_apply=%region_6.7 | all-reduce | flops 2 | bytes 16 | tf_op jit(solution)/shard_map/psum | solution.py:178
  356.2 1.9 fusion.226
  358.2 2.0 collective-permute-start.14
  360.2 3.8 collective-permute-start.15
  364.1 2.0 collective-permute-done.15
  367.8 8.2 %collective-permute-start.16 = (f32[2,1,64,128]{3,2,1,0:T(8,128)S(1)}, f32[2,1,64,128]{3,2,1,0:T(8,128)S(1)}, u32[]{:S(2)}, u32[]{:S(2)}) collective-permute-start(f32[2,1,64,128]{3,2,1,0:T(8,128)S(1)} %get-tuple-element.60), channel_id=1, source_target_pairs={{1,0},{2,1},{3,2},{4,3},{5,4},{6,5},{7,6},{8,7},{9,8},{10,9},{11,1... | collective-permute-start | bytes 196616 | tf_op jit(solution)/shard_map/ppermute | solution.py:29
  376.0 1.9 collective-permute-start.17
  377.9 4.2 collective-permute-done.17
  382.7 1.3 broadcast_multiply_fusion.3
  384.1 6.1 collective-permute-start.18
  390.2 1.9 collective-permute-start.19
  392.2 4.2 collective-permute-done.19
  397.0 1.2 broadcast_multiply_fusion.2
  398.2 6.1 collective-permute-start.20
  404.4 1.9 collective-permute-start.21
  406.3 4.2 collective-permute-done.21
  411.1 1.2 fusion.187
  412.3 6.1 collective-permute-start.22
  418.5 2.1 collective-permute-start.23
  420.6 4.0 collective-permute-done.23
  425.2 2.6 broadcast_multiply_fusion.4
  427.8 6.1 collective-permute-start.24
  434.0 1.9 collective-permute-start.25
  435.9 4.2 collective-permute-done.25
  440.8 1.8 fusion.19
  442.5 79.4 %all-reduce.21.cloned.1.call-done = f32[12,64,128]{2,1,0:T(8,128)} async-done(((f32[12,64,128]{2,1,0:T(8,128)}), f32[12,64,128]{2,1,0:T(8,128)}) %all-reduce.21.cloned.1.call-update) | async-done | bytes 393232 | tf_op jit(solution)/shard_map/psum | solution.py:173
  521.9 1.0 fusion.191
  523.0 2.5 collective-permute-start.26
  525.4 3.4 collective-permute-start.27
  528.8 3.0 collective-permute-done.27
  532.2 1.1 abs_reduce_fusion
  533.2 159.2 %all-reduce.14 = (f32[]{:T(128)}, f32[]{:T(128)}) all-reduce(f32[]{:T(128)} %get-tuple-element.9, f32[]{:T(128)} %get-tuple-element.7), channel_id=1, replica_groups=mesh['load'=8,'brick'=64] {'brick'}, use_global_device_ids=true, to_apply=%region_12.13 | all-reduce | flops 2 | bytes 16 | tf_op jit(solution)/shard_map/psum | solution.py:178
  694.4 1.4 fusion.220
  (100 shorter events, 12.6 us)
Async XLA Ops:
  7.2 8.6 %copy-start.16 = (s32[2,64]{1,0:T(2,128)S(1)}, s32[2,64]{1,0:T(2,128)}, u32[]{:S(2)}) copy-start(s32[2,64]{1,0:T(2,128)} %param.10) | copy-start | bytes 1540
  7.2 8.7 %copy-start.17 = (f32[2,64]{1,0:T(2,128)S(1)}, f32[2,64]{1,0:T(2,128)}, u32[]{:S(2)}) copy-start(f32[2,64]{1,0:T(2,128)} %param.11) | copy-start | bytes 1540
  7.2 176.5 %all-reduce.19.cloned.1.call-start = ((), (), s32[]{:S(2)}) async-start(), calls=%async_computation | async-start | bytes 786432 | tf_op jit(solution)/shard_map/psum | solution.py:173
  9.9 13.4 %collective-permute-start = (f32[1,64,128]{2,1,0:T(8,128)S(1)}, f32[1,64,128]{2,1,0:T(8,128)S(1)}, u32[]{:S(2)}, u32[]{:S(2)}) collective-permute-start(f32[1,64,128]{2,1,0:T(8,128)S(1)} %get-tuple-element.83), channel_id=1, source_target_pairs={{1,0},{2,1},{3,2},{4,3},{5,4},{6,5},{7,6},{8,7},{9,8},{10,9},{11,1... | collective-permute-start | bytes 98312 | tf_op jit(solution)/shard_map/ppermute | solution.py:29
  12.4 11.0 %collective-permute-start.1 = (f32[1,64,128]{2,1,0:T(8,128)S(1)}, f32[1,64,128]{2,1,0:T(8,128)S(1)}, u32[]{:S(2)}, u32[]{:S(2)}) collective-permute-start(f32[1,64,128]{2,1,0:T(8,128)S(1)} %get-tuple-element.82), channel_id=1, source_target_pairs={{0,1},{1,2},{2,3},{3,4},{4,5},{5,6},{6,7},{7,8},{8,9},{9,10},{10,1... | collective-permute-start | bytes 98312 | tf_op jit(solution)/shard_map/ppermute | solution.py:26
  16.2 7.1 %copy-start.5 = (s32[12,64,128]{2,1,0:T(8,128)S(1)}, s32[12,64,128]{2,1,0:T(8,128)}, u32[]{:S(2)}) copy-start(s32[12,64,128]{2,1,0:T(8,128)} %param.9) | copy-start | bytes 1179652
  23.2 1.7 copy-start.6
  23.4 0.6 copy-start.9
  24.0 0.6 copy-start.10
  24.9 1.5 copy-start
  25.0 1.5 copy-start.11
  26.5 0.8 copy-start.3
  26.5 15.1 %copy-start.1 = (f32[12,64,128]{2,1,0:T(8,128)}, f32[12,64,128]{2,1,0:T(8,128)S(1)}, u32[]{:S(2)}) copy-start(f32[12,64,128]{2,1,0:T(8,128)S(1)} %get-tuple-element.72) | copy-start | bytes 1179652
  27.2 6.2 collective-permute-start.2
  30.5 10.4 %collective-permute-start.3 = (f32[2,1,64,128]{3,2,1,0:T(8,128)S(1)}, f32[2,1,64,128]{3,2,1,0:T(8,128)S(1)}, u32[]{:S(2)}, u32[]{:S(2)}) collective-permute-start(f32[2,1,64,128]{3,2,1,0:T(8,128)S(1)} %get-tuple-element.69), channel_id=1, source_target_pairs={{0,1},{1,2},{2,3},{3,4},{4,5},{5,6},{6,7},{7,8},{8,9},{9,10},{10,1... | collective-permute-start | bytes 196616 | tf_op jit(solution)/shard_map/ppermute | solution.py:26
  42.9 10.1 %collective-permute-start.4 = (f32[2,1,64,128]{3,2,1,0:T(8,128)S(1)}, f32[2,1,64,128]{3,2,1,0:T(8,128)S(1)}, u32[]{:S(2)}, u32[]{:S(2)}) collective-permute-start(f32[2,1,64,128]{3,2,1,0:T(8,128)S(1)} %get-tuple-element.68), channel_id=1, source_target_pairs={{1,0},{2,1},{3,2},{4,3},{5,4},{6,5},{7,6},{8,7},{9,8},{10,9},{11,1... | collective-permute-start | bytes 196616 | tf_op jit(solution)/shard_map/ppermute | solution.py:29
  51.0 6.2 collective-permute-start.5
  59.0 8.1 %collective-permute-start.6 = (f32[2,1,64,128]{3,2,1,0:T(8,128)S(1)}, f32[2,1,64,128]{3,2,1,0:T(8,128)S(1)}, u32[]{:S(2)}, u32[]{:S(2)}) collective-permute-start(f32[2,1,64,128]{3,2,1,0:T(8,128)S(1)} %get-tuple-element.66), channel_id=1, source_target_pairs={{1,0},{2,1},{3,2},{4,3},{5,4},{6,5},{7,6},{8,7},{9,8},{10,9},{11,1... | collective-permute-start | bytes 196616 | tf_op jit(solution)/shard_map/ppermute | solution.py:29
  65.2 6.2 collective-permute-start.7
  73.1 8.1 %collective-permute-start.8 = (f32[2,1,64,128]{3,2,1,0:T(8,128)S(1)}, f32[2,1,64,128]{3,2,1,0:T(8,128)S(1)}, u32[]{:S(2)}, u32[]{:S(2)}) collective-permute-start(f32[2,1,64,128]{3,2,1,0:T(8,128)S(1)} %get-tuple-element.64), channel_id=1, source_target_pairs={{1,0},{2,1},{3,2},{4,3},{5,4},{6,5},{7,6},{8,7},{9,8},{10,9},{11,1... | collective-permute-start | bytes 196616 | tf_op jit(solution)/shard_map/ppermute | solution.py:29
  79.2 6.2 collective-permute-start.9
  87.8 8.3 %collective-permute-start.10 = (f32[2,1,64,128]{3,2,1,0:T(8,128)S(1)}, f32[2,1,64,128]{3,2,1,0:T(8,128)S(1)}, u32[]{:S(2)}, u32[]{:S(2)}) collective-permute-start(f32[2,1,64,128]{3,2,1,0:T(8,128)S(1)} %get-tuple-element.62), channel_id=1, source_target_pairs={{1,0},{2,1},{3,2},{4,3},{5,4},{6,5},{7,6},{8,7},{9,8},{10,9},{11,1... | collective-permute-start | bytes 196616 | tf_op jit(solution)/shard_map/ppermute | solution.py:29
  93.9 6.2 collective-permute-start.11
  102.5 419.4 %all-reduce.21.cloned.1.call-start = ((), (), s32[]{:S(2)}) async-start(), calls=%async_computation.1 | async-start | bytes 786432 | tf_op jit(solution)/shard_map/psum | solution.py:173
  102.6 91.3 %copy-start.12 = (f32[64]{0:T(128)}, f32[64]{0:T(128)S(1)}, u32[]{:S(2)}) copy-start(f32[64]{0:T(128)S(1)} %get-tuple-element.87) | copy-start | bytes 772
  184.7 5.9 collective-permute-start.12
  187.2 6.4 collective-permute-start.13
  190.6 3.3 copy-start.14
  195.7 170.6 %copy-start.7 = (s32[12,64,128]{2,1,0:T(8,128)S(1)}, s32[12,64,128]{2,1,0:T(8,128)}, u32[]{:S(2)}) copy-start(s32[12,64,128]{2,1,0:T(8,128)} %param.9) | copy-start | bytes 1179652
  358.2 5.9 collective-permute-start.14
  360.2 5.8 collective-permute-start.15
  366.4 1.0 copy-start.4
  367.7 15.0 %copy-start.2 = (f32[12,64,128]{2,1,0:T(8,128)S(1)}, f32[12,64,128]{2,1,0:T(8,128)}, u32[]{:S(2)}) copy-start(f32[12,64,128]{2,1,0:T(8,128)} %copy-done.1) | copy-start | bytes 1179652
  367.8 10.1 %collective-permute-start.16 = (f32[2,1,64,128]{3,2,1,0:T(8,128)S(1)}, f32[2,1,64,128]{3,2,1,0:T(8,128)S(1)}, u32[]{:S(2)}, u32[]{:S(2)}) collective-permute-start(f32[2,1,64,128]{3,2,1,0:T(8,128)S(1)} %get-tuple-element.60), channel_id=1, source_target_pairs={{1,0},{2,1},{3,2},{4,3},{5,4},{6,5},{7,6},{8,7},{9,8},{10,9},{11,1... | collective-permute-start | bytes 196616 | tf_op jit(solution)/shard_map/ppermute | solution.py:29
  376.0 6.2 collective-permute-start.17
  384.1 8.1 %collective-permute-start.18 = (f32[2,1,64,128]{3,2,1,0:T(8,128)S(1)}, f32[2,1,64,128]{3,2,1,0:T(8,128)S(1)}, u32[]{:S(2)}, u32[]{:S(2)}) collective-permute-start(f32[2,1,64,128]{3,2,1,0:T(8,128)S(1)} %get-tuple-element.58), channel_id=1, source_target_pairs={{1,0},{2,1},{3,2},{4,3},{5,4},{6,5},{7,6},{8,7},{9,8},{10,9},{11,1... | collective-permute-start | bytes 196616 | tf_op jit(solution)/shard_map/ppermute | solution.py:29
  390.2 6.2 collective-permute-start.19
  398.2 8.1 %collective-permute-start.20 = (f32[2,1,64,128]{3,2,1,0:T(8,128)S(1)}, f32[2,1,64,128]{3,2,1,0:T(8,128)S(1)}, u32[]{:S(2)}, u32[]{:S(2)}) collective-permute-start(f32[2,1,64,128]{3,2,1,0:T(8,128)S(1)} %get-tuple-element.56), channel_id=1, source_target_pairs={{1,0},{2,1},{3,2},{4,3},{5,4},{6,5},{7,6},{8,7},{9,8},{10,9},{11,1... | collective-permute-start | bytes 196616 | tf_op jit(solution)/shard_map/ppermute | solution.py:29
  404.4 6.2 collective-permute-start.21
  412.3 8.3 %collective-permute-start.22 = (f32[2,1,64,128]{3,2,1,0:T(8,128)S(1)}, f32[2,1,64,128]{3,2,1,0:T(8,128)S(1)}, u32[]{:S(2)}, u32[]{:S(2)}) collective-permute-start(f32[2,1,64,128]{3,2,1,0:T(8,128)S(1)} %get-tuple-element.54), channel_id=1, source_target_pairs={{1,0},{2,1},{3,2},{4,3},{5,4},{6,5},{7,6},{8,7},{9,8},{10,9},{11,1... | collective-permute-start | bytes 196616 | tf_op jit(solution)/shard_map/ppermute | solution.py:29
  418.5 6.2 collective-permute-start.23
  427.8 8.1 %collective-permute-start.24 = (f32[2,1,64,128]{3,2,1,0:T(8,128)S(1)}, f32[2,1,64,128]{3,2,1,0:T(8,128)S(1)}, u32[]{:S(2)}, u32[]{:S(2)}) collective-permute-start(f32[2,1,64,128]{3,2,1,0:T(8,128)S(1)} %get-tuple-element.52), channel_id=1, source_target_pairs={{1,0},{2,1},{3,2},{4,3},{5,4},{6,5},{7,6},{8,7},{9,8},{10,9},{11,1... | collective-permute-start | bytes 196616 | tf_op jit(solution)/shard_map/ppermute | solution.py:29
  434.0 6.2 collective-permute-start.25
  442.5 89.6 %copy-start.8 = (f32[12,64,128]{2,1,0:T(8,128)S(1)}, f32[12,64,128]{2,1,0:T(8,128)}, u32[]{:S(2)}) copy-start(f32[12,64,128]{2,1,0:T(8,128)} %get-tuple-element.26) | copy-start | bytes 1179652
  442.5 89.7 %copy-start.13 = (f32[64]{0:T(128)S(1)}, f32[64]{0:T(128)}, u32[]{:S(2)}) copy-start(f32[64]{0:T(128)} %copy-done.12) | copy-start | bytes 772
  442.5 89.7 %copy-start.15 = (f32[12]{0:T(128)S(1)}, f32[12]{0:T(128)}, u32[]{:S(2)}) copy-start(f32[12]{0:T(128)} %copy-done.14) | copy-start | bytes 148
  523.0 5.9 collective-permute-start.26
  525.4 6.4 collective-permute-start.27
Sparse Core Ops, SparseCore 0:
  102.6 80.9 all-reduce.18
  442.7 79.1 all-reduce.20
where the time goes:
time: 704 us; the launch traced here: 703 us
  blocking collectives  318 us (45%)
  waiting for transfers between devices  214 us (30%)
  starting transfers between devices  106 us (15%)
  other arithmetic  43.3 us (6%)
  between operations  17.6 us (3%)
    psum x2, blocking collectives, body(): lax.psum((jnp.sum(jnp.abs(momentum)), jnp.sum(design_here)), 'brick')  318 us
    psum x2, waiting for transfers between devices, body(): energy = lax.psum(local_energy, 'load')  160 us
    ppermute x14, starting transfers between devices, padded_2(): lax.ppermute(lax.slice_in_dim(block, 0, width, axis=dim), axis, backward)  72 us
    ppermute x14, waiting for transfers between devices, padded_2(): lax.ppermute(lax.slice_in_dim(block, block.shape[dim] - width, None, axis...  53 us
    ppermute x14, starting transfers between devices, padded_2(): lax.ppermute(lax.slice_in_dim(block, block.shape[dim] - width, None, axis...  34.2 us
  transfers between devices with their start and end apart: 30, of which 16 were waited for; matrix products, arithmetic and copies ran while one was open for 1% of the time, Pallas kernels for 0%

commit v1 on v0

v1 whole, which is shorter than its diff:
```python
import functools

import jax
import jax.numpy as jnp
from jax import lax
from jax.experimental import pallas as pl
from jax.experimental.pallas import tpu as pltpu
from jax.sharding import PartitionSpec as P

SWEEPS = 5
DESIGN_ITERS = 2
HALO = 7
WIDE = HALO - 1
XS, YLS, CORES = 4, 2, 2

stiff_floor = 0.01
mass_shift = 0.1
spectrum_low = 0.05
spectrum_high = 2.0
moment_decay = 0.8
step_size = 0.1
volume_pull = 0.5
volume_target = 0.4
density_floor = 0.001

F32 = jnp.float32


def chebyshev_factors():
    centre = 0.5 * (spectrum_high + spectrum_low)
    half_width = 0.5 * (spectrum_high - spectrum_low)
    ratio_one = centre / half_width
    previous = 1.0 / ratio_one
    factors = []
    for _ in range(SWEEPS - 1):
        current = 1.0 / (2.0 * ratio_one - previous)
        factors.append((current * previous, 2.0 * current / half_width))
        previous = current
    return 1.0 / centre, factors


def passive_apply(design, passive):
    return jnp.where(passive == 1, density_floor, jnp.where(passive == 2, 1.0, design))


def kernel(
    dims,
    density_ref, passive_ref, support_ref, nodes_ref, force_ref, weight_ref, body_ref,
    new_ref, moment_ref, disp_ref,
    design, support, passive, source, stiff, coef, gain, direct, resid, sens, moved_x,
    part, pair_in, pair_out, row_in, filt, msg, slots_one, slots_two,
    load_sems, body_send, body_recv, sup_send, sup_recv, supf_send, supf_recv,
    des_send, des_recv, desf_send, desf_recv,
    pair_send, pair_recv, row_send, row_recv, gath_send, gath_recv, gatf_send, gatf_recv,
    one_send, one_recv, two_send, two_recv, disp_sem,
):
    loads, bricks, cells_x, size_y, size_z, nodes = dims
    rows_hi = loads // CORES
    zs = bricks // (XS * YLS)
    slab = size_y // loads
    half = size_y // CORES
    ext = cells_x + 2 * HALO
    total_x = bricks * cells_x
    total_cells = float(total_x * size_y * size_z)
    last = HALO + cells_x
    local_loads = body_ref.shape[0]

    load = lax.axis_index("load")
    brick = lax.axis_index("brick")
    core = lax.rem(load, CORES)
    row = load // CORES
    at_x = lax.rem(brick, XS)
    at_yl = lax.rem(brick // XS, YLS)
    at_z = brick // (XS * YLS)
    has_low = brick > 0
    has_high = brick < bricks - 1
    partner = {"load": row * CORES + 1 - core, "brick": brick}

    def device(load_index, brick_index):
        return {"load": load_index, "brick": brick_index}

    group_one = rows_hi * YLS * CORES
    me_one = (row * YLS + at_yl) * CORES + core
    group_two = zs * XS
    me_two = at_z * XS + at_x

    def member_one(index):
        other_core = lax.rem(index, CORES)
        other_yl = lax.rem(index // CORES, YLS)
        other_row = index // (CORES * YLS)
        return device(other_row * CORES + other_core, (at_z * YLS + other_yl) * XS + at_x)

    def member_two(index):
        return device(load, (index // XS * YLS + at_yl) * XS + lax.rem(index, XS))

    def remote(src, dst, send, recv, target):
        return pltpu.make_async_remote_copy(
            src_ref=src, dst_ref=dst, send_sem=send, recv_sem=recv,
            device_id=target, device_id_type=pl.DeviceIdType.MESH,
        )

    own = pl.ds(HALO, cells_x)
    loads_in = [
        pltpu.make_async_copy(density_ref, design.at[0, own], load_sems.at[0]),
        pltpu.make_async_copy(passive_ref, passive, load_sems.at[1]),
        pltpu.make_async_copy(support_ref, support.at[own], load_sems.at[2]),
        pltpu.make_async_copy(body_ref, source.at[:, own], load_sems.at[3]),
    ]
    for copy in loads_in:
        copy.start()

    barrier = pltpu.get_barrier_semaphore()

    def greet_one(k, carry):
        pl.semaphore_signal(barrier, 1, device_id=member_one(lax.rem(me_one + k, group_one)),
                            device_id_type=pl.DeviceIdType.MESH)
        return carry

    def greet_two(k, carry):
        pl.semaphore_signal(barrier, 1, device_id=member_two(lax.rem(me_two + k, group_two)),
                            device_id_type=pl.DeviceIdType.MESH)
        return carry

    @pl.when(has_low)
    def _():
        pl.semaphore_signal(barrier, 1, device_id=device(load, brick - 1),
                            device_id_type=pl.DeviceIdType.MESH)

    @pl.when(has_high)
    def _():
        pl.semaphore_signal(barrier, 1, device_id=device(load, brick + 1),
                            device_id_type=pl.DeviceIdType.MESH)

    lax.fori_loop(1, group_two, greet_two, 0)
    lax.fori_loop(1, group_one, greet_one, 0)
    sides = jnp.where(has_low, 1, 0) + jnp.where(has_high, 1, 0)
    pl.semaphore_wait(barrier, group_one + group_two - 2 + sides)

    low, high = device(load, brick - 1), device(load, brick + 1)
    mine = pl.ds(pl.multiple_of(core * half, half), half)
    others = pl.ds(pl.multiple_of((1 - core) * half, half), half)

    def halo_copies(src, src_first, dst, width, send, recv, lead, rows):
        cut = (lambda ref, first: ref.at[lead + (pl.ds(first, width),) + rows])
        down = remote(cut(src, src_first), cut(dst, last), send.at[0], recv.at[1], low)
        up = remote(cut(src, src_first + cells_x - width), cut(dst, HALO - width),
                    send.at[1], recv.at[0], high)
        return down, up

    def start_halo(copies):
        down, up = copies

        @pl.when(has_low)
        def _():
            down.start()

        @pl.when(has_high)
        def _():
            up.start()

    def landed(dst, width, recv, send, lead, rows, side):
        first = HALO - width if side == 0 else last
        ref = dst.at[lead + (pl.ds(first, width),) + rows]
        return remote(ref, ref, send.at[side], recv.at[side], partner)

    body_rows = (slice(None), slice(None))
    body_copies = halo_copies(body_ref, 0, source, WIDE, body_send, body_recv, (slice(None),), body_rows)
    start_halo(body_copies)
    sup_copies = halo_copies(support_ref, 0, support, WIDE, sup_send, sup_recv, (), (mine, slice(None)))
    start_halo(sup_copies)

    loads_in[0].wait()
    loads_in[1].wait()

    def first_design(layer, carry):
        design[0, layer + HALO] = passive_apply(design[0, layer + HALO], passive[layer])
        return carry

    lax.fori_loop(0, cells_x, first_design, 0)

    def send_design(step):
        copies = halo_copies(design, HALO, design, HALO, des_send.at[step], des_recv.at[step],
                             (step,), (mine, slice(None)))
        start_halo(copies)
        return copies

    def clear(first):
        zero = jnp.zeros((size_y, size_z), F32)
        for layer in range(first, first + HALO):
            for step in range(DESIGN_ITERS):
                design[step, layer] = zero
            support[layer] = jnp.ones((size_y, size_z), jnp.int32)
            for one in range(local_loads):
                source[one, layer] = zero

    @pl.when(jnp.logical_not(has_low))
    def _():
        clear(0)

    @pl.when(jnp.logical_not(has_high))
    def _():
        clear(last)

    design_copies = [send_design(0)]
    loads_in[2].wait()
    loads_in[3].wait()

    node = nodes_ref[...]
    node_row = lax.shift_right_logical(node, size_z.bit_length() - 1)
    node_col = lax.bitwise_and(node, size_z - 1)
    flat_rows = jnp.concatenate([node_row[i:i + 1] for i in range(local_loads)], axis=1)
    flat_cols = jnp.concatenate([node_col[i:i + 1] for i in range(local_loads)], axis=1)
    flat_force = jnp.concatenate([force_ref[i:i + 1] for i in range(local_loads)], axis=1)
    width = local_loads * nodes
    col_of = jnp.transpose(jnp.broadcast_to(flat_cols.astype(F32), (size_z, width)))
    force_of = jnp.transpose(jnp.broadcast_to(flat_force, (size_z, width)))
    lanes = lax.broadcasted_iota(jnp.int32, (width, size_z), 1).astype(F32)
    owner = lax.broadcasted_iota(jnp.int32, (width, size_z), 0) // nodes
    placed = jnp.where(lanes == col_of, force_of, 0.0)
    spread = jnp.concatenate(
        [jnp.where(owner == i, placed, 0.0) for i in range(local_loads)], axis=1
    )
    row_iota = lax.broadcasted_iota(jnp.int32, (size_y, width), 0)

    def add_points(layer, carry):
        base = (brick * cells_x + layer - HALO) * size_y
        hot = jnp.where(row_iota + base == flat_rows, 1.0, 0.0)
        found = jnp.dot(hot, spread, preferred_element_type=F32, precision=lax.Precision.HIGHEST)
        for one in range(local_loads):
            source[one, layer] = source[one, layer] + found[:, one * size_z:(one + 1) * size_z]
        return carry

    iota_y = lax.broadcasted_iota(jnp.int32, (size_y, size_z), 0)
    iota_z = lax.broadcasted_iota(jnp.int32, (size_y, size_z), 1)
    y_first, y_last = iota_y == 0, iota_y == size_y - 1
    z_first, z_last = iota_z == 0, iota_z == size_z - 1

    def y_up(value):
        return pltpu.roll(value, size_y - 1, 0)

    def y_down(value):
        return pltpu.roll(value, 1, 0)

    def z_up(value):
        return pltpu.roll(value, size_z - 1, 1)

    def z_down(value):
        return pltpu.roll(value, 1, 1)

    def inner_sides(value):
        return (
            jnp.where(y_last, 0.0, y_up(value)),
            jnp.where(y_first, 0.0, y_down(value)),
            jnp.where(z_last, 0.0, z_up(value)),
            jnp.where(z_first, 0.0, z_down(value)),
        )

    first_scale, factors = chebyshev_factors()

    def run(first, stop, body):
        lax.fori_loop(first + HALO, stop + HALO, lambda e, c: (body(e), c)[1], 0)

    def make_stiff(step):
        def body(e):
            at = brick * cells_x + e - HALO
            inside = jnp.where(jnp.logical_and(at >= 0, at < total_x), 1.0, 0.0).astype(F32)
            value = design[step, e]
            stiff[e] = inside * (stiff_floor + (1.0 - stiff_floor) * (value * value * value))
        return body

    def make_coef(step):
        def body(e):
            s = stiff[e]
            free = (1 - support[e]).astype(F32)
            sides = (stiff[e + 1], stiff[e - 1]) + inner_sides(s)
            faces = [0.5 * (s + side) for side in sides]
            total = faces[0]
            for face in faces[1:]:
                total = total + face
            scale = free / (free * (total + mass_shift * s) + (1.0 - free))
            outer = (None, None, y_last, y_first, z_last, z_first)
            for j in range(6):
                value = scale * faces[j]
                coef[j, e] = value if outer[j] is None else jnp.where(outer[j], 0.0, value)
            here = design[step, e]
            for one in range(local_loads):
                start = scale * (source[one, e] + weight_ref[one] * here)
                resid[one, e] = start
                direct[one, 0, e] = first_scale * start
        return body

    def make_sweep(k):
        keep, pull = factors[k]

        def body(e):
            c = [coef[j, e] for j in range(6)]
            for one in range(local_loads):
                d = direct[one, k, e]
                total = c[0] * direct[one, k, e + 1] + c[1] * direct[one, k, e - 1]
                total = total + (c[2] * y_up(d) + c[3] * y_down(d))
                total = total + (c[4] * z_up(d) + c[5] * z_down(d))
                left = (resid[one, e] - d) + total
                if k < SWEEPS - 2:
                    resid[one, e] = left
                    direct[one, k + 1, e] = keep * d + pull * left
                else:
                    full = keep * d + pull * left + d
                    for older in range(k):
                        full = full + direct[one, older, e]
                    moved_x[one, e] = full
        return body

    def make_sens(step):
        def body(e):
            total = None
            for one in range(local_loads):
                f = moved_x[one, e]
                gaps = None
                for beside in (moved_x[one, e + 1], moved_x[one, e - 1]) + inner_sides(f):
                    gap = f - beside
                    gaps = gap * gap if gaps is None else gaps + gap * gap
                value = mass_shift * (f * f) + 0.25 * gaps
                total = value if total is None else total + value
            here = design[step, e]
            sens[e] = (-3.0 * (1.0 - stiff_floor)) * (here * here) * total
        return body

    edge_count = (
        y_first.astype(F32) + y_last.astype(F32) + z_first.astype(F32) + z_last.astype(F32)
    )

    def filter_layer(e):
        at = brick * cells_x + e - HALO
        end = jnp.where(jnp.logical_or(at == 0, at == total_x - 1), 1.0, 0.0).astype(F32)
        value = sens[e]
        total = 2.0 * value + sens[e + 1] + sens[e - 1]
        for beside in inner_sides(value):
            total = total + beside
        part[e - HALO] = total / (8.0 - (edge_count + end))

    def slab_rows(index):
        return pl.ds(pl.multiple_of(index * slab, slab), slab)

    def other_row(k):
        return lax.rem(row + k, rows_hi)

    my_slab = slab_rows(load)

    for step in range(DESIGN_ITERS):
        final = step == DESIGN_ITERS - 1
        run(0, cells_x, make_stiff(step))
        if step == 0:
            run(0, cells_x, lambda e: add_points(e, 0))
        run(1, cells_x - 1, make_coef(step))
        for k in range(SWEEPS - 1):
            run(2 + k, cells_x - 2 - k, make_sweep(k))

        for side, there in ((0, has_low), (1, has_high)):
            first = HALO - WIDE if side == 0 else last

            @pl.when(there)
            def _(side=side, there=there, first=first, step=step):
                if step == 0:
                    landed(support, WIDE, sup_recv, sup_send, (), (mine, slice(None)), side).wait_recv()
                    ref = support.at[pl.ds(first, WIDE), mine]
                    remote(ref, ref, supf_send.at[side], supf_recv.at[side], partner).start()
                landed(design, HALO, des_recv.at[step], des_send.at[step], (step,), (mine, slice(None)), side).wait_recv()
                ref = design.at[step, pl.ds(0 if side == 0 else last, HALO), mine]
                remote(ref, ref, desf_send.at[step, side], desf_recv.at[step, side], partner).start()
                if step == 0:
                    landed(source, WIDE, body_recv, body_send, (slice(None),), body_rows, side).wait_recv()
                    ref = support.at[pl.ds(first, WIDE), others]
                    remote(ref, ref, supf_send.at[side], supf_recv.at[side], partner).wait_recv()
                ref = design.at[step, pl.ds(0 if side == 0 else last, HALO), others]
                remote(ref, ref, desf_send.at[step, side], desf_recv.at[step, side], partner).wait_recv()

        for side in (0, 1):
            low_end = (lambda a, b: (a, b)) if side == 0 else (lambda a, b: (cells_x - b, cells_x - a))
            run(*low_end(-HALO, 0), make_stiff(step))
            if step == 0:
                run(*low_end(-WIDE, 0), lambda e: add_points(e, 0))
            run(*low_end(-WIDE, 1), make_coef(step))
        for side in (0, 1):
            low_end = (lambda a, b: (a, b)) if side == 0 else (lambda a, b: (cells_x - b, cells_x - a))
            for k in range(SWEEPS - 1):
                run(*low_end(k + 1 - WIDE, 2 + k), make_sweep(k))
        if final:
            out_copy = pltpu.make_async_copy(moved_x.at[:, own], disp_ref, disp_sem)
            out_copy.start()
        run(-1, cells_x + 1, make_sens(step))
        run(0, cells_x, filter_layer)

        to_pair = []
        for k in range(rows_hi):
            index = other_row(k)
            rows = slab_rows(index * CORES + 1 - core)
            copy = remote(part.at[:, rows], pair_in.at[step, index], pair_send.at[step, k],
                          pair_recv.at[step, index], partner)
            copy.start()
            to_pair.append(copy)
        to_row = []
        order = sorted(range(1, rows_hi), key=lambda k: -min(k, rows_hi - k)) + [0]
        for k in order:
            index = other_row(k)
            rows = slab_rows(index * CORES + core)
            remote(part.at[:, rows], pair_in.at[step, index], pair_send.at[step, k],
                   pair_recv.at[step, index], partner).wait_recv()
            pair_out[step, k] = part[:, rows] + pair_in[step, index]
            if k:
                copy = remote(pair_out.at[step, k], row_in.at[step, k], row_send.at[step, k],
                              row_recv.at[step, k], device(index * CORES + core, brick))
                copy.start()
                to_row.append(copy)
        total = pair_out[step, 0]
        for copy, k in zip(to_row, order):
            copy.wait_recv()
            total = total + row_in[step, k]
        if final:
            total = moment_decay * filt[:, my_slab] + total
            moment_ref[...] = total
        else:
            filt[:, my_slab] = total

        here = design[step, own, my_slab]
        msg[step, 0] = jnp.concatenate(
            [jnp.sum(jnp.abs(total), axis=0), jnp.sum(here, axis=0)], axis=0)
        slots_one[step, me_one] = msg[step, 0]

        def copy_one(k):
            index = lax.rem(me_one + k, group_one)
            return remote(msg.at[step, 0], slots_one.at[step, me_one], one_send.at[step, k],
                          one_recv.at[step, me_one], member_one(index))

        def came_one(k):
            index = lax.rem(me_one + k, group_one)
            return remote(msg.at[step, 0], slots_one.at[step, index], one_send.at[step, k],
                          one_recv.at[step, index], member_one(index))

        def copy_two(k):
            index = lax.rem(me_two + k, group_two)
            return remote(msg.at[step, 1], slots_two.at[step, me_two], two_send.at[step, k],
                          two_recv.at[step, me_two], member_two(index))

        def came_two(k):
            index = lax.rem(me_two + k, group_two)
            return remote(msg.at[step, 1], slots_two.at[step, index], two_send.at[step, k],
                          two_recv.at[step, index], member_two(index))

        def each(count, action):
            lax.fori_loop(1, count, lambda k, c: (action(k), c)[1], 0)

        each(group_one, lambda k: copy_one(k).start())

        gathers = []
        if not final:
            for k in order[:-1]:
                index = other_row(k)
                copy = remote(filt.at[:, my_slab], filt.at[:, my_slab], gath_send.at[k],
                              gath_recv.at[k], device(index * CORES + core, brick))
                copy.start()
                gathers.append(copy)
            copy = remote(filt.at[:, my_slab], filt.at[:, my_slab], gatf_send.at[0],
                          gatf_recv.at[0], partner)
            copy.start()
            gathers.append(copy)

        each(group_one, lambda k: came_one(k).wait_recv())
        msg[step, 1] = jnp.sum(slots_one[step], axis=0)
        slots_two[step, me_two] = msg[step, 1]
        each(group_two, lambda k: copy_two(k).start())

        if not final:
            for k in order[:-1][::-1]:
                index = lax.rem(row + rows_hi - k, rows_hi)
                ref = filt.at[:, slab_rows(index * CORES + core)]
                remote(ref, ref, gath_send.at[k], gath_recv.at[k], partner).wait_recv()
                copy = remote(ref, ref, gatf_send.at[k], gatf_recv.at[k], partner)
                copy.start()
                gathers.append(copy)
            for k in [0] + order[:-1][::-1]:
                index = lax.rem(row + rows_hi - k, rows_hi)
                ref = filt.at[:, slab_rows(index * CORES + 1 - core)]
                remote(ref, ref, gatf_send.at[k], gatf_recv.at[k], partner).wait_recv()

        each(group_two, lambda k: came_two(k).wait_recv())
        sums = jnp.sum(slots_two[step], axis=0)
        abs_total = jnp.sum(sums[0:slab], keepdims=True)
        density_total = jnp.sum(sums[slab:2 * slab], keepdims=True)
        rate = step_size / (abs_total / total_cells + 1e-06)
        pull_down = volume_pull * (density_total / total_cells - volume_target)

        def updated(old, moment, kind):
            value = old - rate * moment - pull_down
            return passive_apply(jnp.clip(value, density_floor, 1.0), kind)

        if final:
            def last_design(layer, carry):
                new_ref[layer] = updated(design[step, layer + HALO, my_slab],
                                         moment_ref[layer], passive[layer, my_slab])
                return carry

            lax.fori_loop(0, cells_x, last_design, 0)
        else:
            def next_design(layer, carry):
                design[step + 1, layer + HALO] = updated(
                    design[step, layer + HALO], filt[layer], passive[layer])
                return carry

            lax.fori_loop(0, cells_x, next_design, 0)
            design_copies.append(send_design(step + 1))

        for copy in to_pair + to_row + gathers:
            copy.wait_send()
        each(group_one, lambda k: copy_one(k).wait_send())
        each(group_two, lambda k: copy_two(k).wait_send())

    for side, there in ((0, has_low), (1, has_high)):
        @pl.when(there)
        def _(side=side):
            body_copies[side].wait_send()
            sup_copies[side].wait_send()
            first = HALO - WIDE if side == 0 else last
            ref = support.at[pl.ds(first, WIDE), mine]
            remote(ref, ref, supf_send.at[side], supf_recv.at[side], partner).wait_send()
            for step in range(DESIGN_ITERS):
                design_copies[step][side].wait_send()
                ref = design.at[step, pl.ds(0 if side == 0 else last, HALO), mine]
                remote(ref, ref, desf_send.at[step, side], desf_recv.at[step, side], partner).wait_send()
    out_copy.wait()


def body(dims, density, passive, support, load_nodes, load_force, self_weight, body_force):
    loads, bricks, cells_x, size_y, size_z, nodes = dims
    local_loads = body_force.shape[0]
    rows_hi = loads // CORES
    zs = bricks // (XS * YLS)
    slab = size_y // loads
    ext = cells_x + 2 * HALO
    group_one, group_two = loads * YLS, zs * XS
    steps = DESIGN_ITERS
    layer = (size_y, size_z)
    vmem = pltpu.VMEM
    dma = pltpu.SemaphoreType.DMA
    space_any = pl.BlockSpec(memory_space=pl.ANY)
    space_vmem = pl.BlockSpec(memory_space=pltpu.VMEM)
    space_smem = pl.BlockSpec(memory_space=pltpu.SMEM)
    piece = (cells_x, slab, size_z)
    return pl.pallas_call(
        functools.partial(kernel, dims),
        out_shape=(
            jax.ShapeDtypeStruct((cells_x, slab, size_z), F32),
            jax.ShapeDtypeStruct((cells_x, slab, size_z), F32),
            jax.ShapeDtypeStruct((local_loads, cells_x) + layer, F32),
        ),
        in_specs=[space_any, space_any, space_any, space_vmem, space_vmem, space_smem, space_any],
        out_specs=(space_vmem, space_vmem, space_any),
        scratch_shapes=[
            vmem((steps, ext) + layer, F32),
            vmem((ext,) + layer, jnp.int32),
            vmem((cells_x,) + layer, jnp.int32),
            vmem((local_loads, ext) + layer, F32),
            vmem((ext,) + layer, F32),
            vmem((6, ext) + layer, F32),
            vmem((1,) + layer, F32),
            vmem((local_loads, SWEEPS - 1, ext) + layer, F32),
            vmem((local_loads, ext) + layer, F32),
            vmem((ext,) + layer, F32),
            vmem((local_loads, ext) + layer, F32),
            vmem((cells_x,) + layer, F32),
            vmem((steps, rows_hi) + piece, F32),
            vmem((steps, rows_hi) + piece, F32),
            vmem((steps, rows_hi) + piece, F32),
            vmem((cells_x,) + layer, F32),
            vmem((steps, 2, 2 * slab, size_z), F32),
            vmem((steps, group_one, 2 * slab, size_z), F32),
            vmem((steps, group_two, 2 * slab, size_z), F32),
            dma((4,)),
            dma((2,)), dma((2,)),
            dma((2,)), dma((2,)), dma((2,)), dma((2,)),
            dma((steps, 2)), dma((steps, 2)), dma((steps, 2)), dma((steps, 2)),
            dma((steps, rows_hi)), dma((steps, rows_hi)),
            dma((steps, rows_hi)), dma((steps, rows_hi)),
            dma((rows_hi,)), dma((rows_hi,)), dma((rows_hi,)), dma((rows_hi,)),
            dma((steps, group_one)), dma((steps, group_one)),
            dma((steps, group_two)), dma((steps, group_two)),
            dma,
        ],
        compiler_params=pltpu.CompilerParams(collective_id=0, has_side_effects=True),
    )(density, passive, support, load_nodes, load_force, self_weight, body_force)


def solution(mesh):
    placed = (
        P("brick", None, None),
        P("brick", None, None),
        P("brick", None, None),
        P("load", None),
        P("load", None),
        P("load"),
        P("load", "brick", None, None),
    )

    def whole(*args):
        loads, bricks = mesh.shape["load"], mesh.shape["brick"]
        cells, size_y, size_z = args[0].shape
        dims = (loads, bricks, cells // bricks, size_y, size_z, args[3].shape[1])
        return jax.shard_map(
            functools.partial(body, dims),
            mesh=mesh,
            in_specs=placed,
            out_specs=(
                P("brick", "load", None),
                P("brick", "load", None),
                P("load", "brick", None, None),
            ),
            check_vma=False,
        )(*args)

    return whole
```

time: 704 us -> 122 us (0.17)
  the two profiles are of different devices: /device:TPU:258 before, /device:TPU:1 now
where the time goes in v1:
time: 122 us; the launch traced here: 121 us
  Pallas kernels  117 us (96%)
  local copies, waits for them, and re-layouts  4.15 us (3%)
    pallas_call x1, Pallas kernels, body(): pl.pallas_call(functools.partial(kernel, dims), out_shape=(jax.ShapeDtype...  117 us
    unnamed x5, local copies, waits for them, and re-layouts  4.15 us

profile of v1, /device:TPU:1, one launch (start us, length us, event | category | flops | bytes accessed | tf_op | source)
XLA Modules:
  0.0 121.5 jit_solution(4119962518429137136)
XLA Ops:
  0.6 116.7 %shard_map.94 = (f32[12,8,128]{2,1,0:T(8,128)}, f32[12,8,128]{2,1,0:T(8,128)}, f32[2,12,64,128]{3,2,1,0:T(8,128)}) custom-call(f32[12,64,128]{2,1,0:T(8,128)} %density_ref.1, s32[12,64,128]{2,1,0:T(8,128)} %passive_ref.1, s32[12,64,128]{2,1,0:T(8,128)} %support_ref.1, s32[2,64]{1,0:T(2,128)} %nodes_ref.1, f32[2,64]{1,0:T(2,128)} %force_ref.1, f32[2]{0:T(128)} %weight_ref.1, ...), custom_call_target="tpu_custom_call" | custom-call | tf_op jit(solution)/shard_map/pallas_call | solution.py:548
  117.3 0.0 copy-start
  117.3 1.4 %copy.13 = f32[12,8,128]{2,1,0:T(8,128)} copy(f32[12,8,128]{2,1,0:T(8,128)} %get-tuple-element.6) | data formatting | bytes 98304
  118.7 0.0 copy-done
  118.7 0.6 copy.14
  119.4 2.1 %copy.15 = f32[2,12,64,128]{3,2,1,0:T(8,128)} copy(f32[2,12,64,128]{3,2,1,0:T(8,128)} %get-tuple-element.8) | data formatting | bytes 1572864
Async XLA Ops:
  117.3 1.4 %copy-start = (f32[12,8,128]{2,1,0:T(8,128)S(1)}, f32[12,8,128]{2,1,0:T(8,128)}, u32[]{:S(2)}) copy-start(f32[12,8,128]{2,1,0:T(8,128)} %get-tuple-element.7) | copy-start | bytes 147460

commit v2 on v1

--- a/solution.py
+++ b/solution.py
@@ -11,6 +11,8 @@
 DESIGN_ITERS = 2
 HALO = 7
 WIDE = HALO - 1
+PIECES = 4
+PAD = 8
 XS, YLS, CORES = 4, 2, 2
 
 stiff_floor = 0.01
@@ -47,12 +49,12 @@
     dims,
     density_ref, passive_ref, support_ref, nodes_ref, force_ref, weight_ref, body_ref,
     new_ref, moment_ref, disp_ref,
-    design, support, passive, source, stiff, coef, gain, direct, resid, sens, moved_x,
+    design, support, passive, source, points, stiff, coef, direct, resid, sens, moved_x,
     part, pair_in, pair_out, row_in, filt, msg, slots_one, slots_two,
     load_sems, body_send, body_recv, sup_send, sup_recv, supf_send, supf_recv,
     des_send, des_recv, desf_send, desf_recv,
     pair_send, pair_recv, row_send, row_recv, gath_send, gath_recv, gatf_send, gatf_recv,
-    one_send, one_recv, two_send, two_recv, disp_sem,
+    one_send, one_recv, two_send, two_recv, disp_sem, hello, column_in, partner_in,
 ):
     loads, bricks, cells_x, size_y, size_z, nodes = dims
     rows_hi = loads // CORES
@@ -110,31 +112,52 @@
         copy.start()
 
     barrier = pltpu.get_barrier_semaphore()
-
-    def greet_one(k, carry):
-        pl.semaphore_signal(barrier, 1, device_id=member_one(lax.rem(me_one + k, group_one)),
-                            device_id_type=pl.DeviceIdType.MESH)
-        return carry
-
-    def greet_two(k, carry):
-        pl.semaphore_signal(barrier, 1, device_id=member_two(lax.rem(me_two + k, group_two)),
-                            device_id_type=pl.DeviceIdType.MESH)
-        return carry
+    size_ring = {"y": YLS * rows_hi, "z": zs}
+
+    def ring_peer(axis, shift):
+        count = size_ring[axis]
+        if axis == "z":
+            there = lax.rem(at_z + shift + count, count)
+            return device(load, (there * YLS + at_yl) * XS + at_x)
+        there = lax.rem(row * YLS + at_yl + shift + count, count)
+        return device(there // YLS * CORES + core, (at_z * YLS + lax.rem(there, YLS)) * XS + at_x)
+
+    def x_peer(shift):
+        return device(load, (at_z * YLS + at_yl) * XS + lax.rem(at_x + shift, XS))
+
+    def signal(semaphore, target):
+        pl.semaphore_signal(semaphore, 1, device_id=target, device_id_type=pl.DeviceIdType.MESH)
 
     @pl.when(has_low)
     def _():
-        pl.semaphore_signal(barrier, 1, device_id=device(load, brick - 1),
-                            device_id_type=pl.DeviceIdType.MESH)
+        signal(barrier, device(load, brick - 1))
 
     @pl.when(has_high)
     def _():
-        pl.semaphore_signal(barrier, 1, device_id=device(load, brick + 1),
-                            device_id_type=pl.DeviceIdType.MESH)
-
-    lax.fori_loop(1, group_two, greet_two, 0)
-    lax.fori_loop(1, group_one, greet_one, 0)
+        signal(barrier, device(load, brick + 1))
+
+    signal(barrier, partner)
+    for shift in range(1, XS):
+        signal(barrier, x_peer(shift))
+    for axis in ("y", "z"):
+        for shift in (1, -1):
+            signal(barrier, ring_peer(axis, shift))
     sides = jnp.where(has_low, 1, 0) + jnp.where(has_high, 1, 0)
-    pl.semaphore_wait(barrier, group_one + group_two - 2 + sides)
+    pl.semaphore_wait(barrier, 1 + (XS - 1) + 4 + sides)
+
+    def pass_on(wave):
+        for i, axis in enumerate(("y", "z")):
+            waves = size_ring[axis] // 2 - 1
+            for j, shift in enumerate((1, -1)):
+                if 0 < wave <= waves:
+                    pl.semaphore_wait(hello.at[i, j, wave - 1], 1)
+                if wave < waves:
+                    signal(hello.at[i, j, wave], ring_peer(axis, -shift))
+
+    def rings_known():
+        for shift in range(1, XS):
+            signal(column_in, x_peer(shift))
+        signal(partner_in, partner)
 
     low, high = device(load, brick - 1), device(load, brick + 1)
     mine = pl.ds(pl.multiple_of(core * half, half), half)
@@ -165,7 +188,6 @@
 
     body_rows = (slice(None), slice(None))
     body_copies = halo_copies(body_ref, 0, source, WIDE, body_send, body_recv, (slice(None),), body_rows)
-    start_halo(body_copies)
     sup_copies = halo_copies(support_ref, 0, support, WIDE, sup_send, sup_recv, (), (mine, slice(None)))
     start_halo(sup_copies)
 
@@ -202,6 +224,23 @@
         clear(last)
 
     design_copies = [send_design(0)]
+    start_halo(body_copies)
+    pass_on(0)
+
+    blank = jnp.zeros((PAD, size_z), F32)
+
+    def clear_pads(layer, carry):
+        for edge in (pl.ds(0, PAD), pl.ds(PAD + size_y, PAD)):
+            stiff[layer, edge] = blank
+            sens[layer, edge] = blank
+            for one in range(local_loads):
+                moved_x[one, layer, edge] = blank
+                for k in range(SWEEPS - 1):
+                    direct[one][k][layer, edge] = blank
+        return carry
+
+    lax.fori_loop(0, ext, clear_pads, 0)
+    pass_on(1)
     loads_in[2].wait()
     loads_in[3].wait()
 
@@ -220,26 +259,32 @@
     spread = jnp.concatenate(
         [jnp.where(owner == i, placed, 0.0) for i in range(local_loads)], axis=1
     )
-    row_iota = lax.broadcasted_iota(jnp.int32, (size_y, width), 0)
-
-    def add_points(layer, carry):
+    batch = 4
+    row_iota = lax.broadcasted_iota(jnp.int32, (batch * size_y, width), 0)
+
+    def find_points(turn, carry):
+        layer = turn * batch + HALO - WIDE
         base = (brick * cells_x + layer - HALO) * size_y
         hot = jnp.where(row_iota + base == flat_rows, 1.0, 0.0)
         found = jnp.dot(hot, spread, preferred_element_type=F32, precision=lax.Precision.HIGHEST)
-        for one in range(local_loads):
-            source[one, layer] = source[one, layer] + found[:, one * size_z:(one + 1) * size_z]
+        for i in range(batch):
+            for one in range(local_loads):
+                points[one, layer + i] = found[
+                    i * size_y:(i + 1) * size_y, one * size_z:(one + 1) * size_z]
         return carry
+
+    assert (cells_x + 2 * WIDE) % batch == 0
+    lax.fori_loop(0, (cells_x + 2 * WIDE) // batch, find_points, 0)
+    pass_on(2)
 
     iota_y = lax.broadcasted_iota(jnp.int32, (size_y, size_z), 0)
     iota_z = lax.broadcasted_iota(jnp.int32, (size_y, size_z), 1)
     y_first, y_last = iota_y == 0, iota_y == size_y - 1
     z_first, z_last = iota_z == 0, iota_z == size_z - 1
-
-    def y_up(value):
-        return pltpu.roll(value, size_y - 1, 0)
-
-    def y_down(value):
-        return pltpu.roll(value, 1, 0)
+    piece_rows = size_y // PIECES
+    rows_in = pl.ds(PAD, size_y)
+    rows_next = pl.ds(PAD + 1, size_y)
+    rows_back = pl.ds(PAD - 1, size_y)
 
     def z_up(value):
         return pltpu.roll(value, size_z - 1, 1)
@@ -247,82 +292,101 @@
     def z_down(value):
         return pltpu.roll(value, 1, 1)
 
-    def inner_sides(value):
-        return (
-            jnp.where(y_last, 0.0, y_up(value)),
-            jnp.where(y_first, 0.0, y_down(value)),
-            jnp.where(z_last, 0.0, z_up(value)),
-            jnp.where(z_first, 0.0, z_down(value)),
-        )
+    def z_sides(value):
+        return jnp.where(z_last, 0.0, z_up(value)), jnp.where(z_first, 0.0, z_down(value))
 
     first_scale, factors = chebyshev_factors()
 
-    def run(first, stop, body):
-        lax.fori_loop(first + HALO, stop + HALO, lambda e, c: (body(e), c)[1], 0)
+    def run(first, stop, body, most=4):
+        count = stop - first
+        group = max(n for n in range(1, most + 1) if count % n == 0)
+
+        def turn(index, carry):
+            for i in range(group):
+                body(first + HALO + index * group + i)
+            return carry
+
+        lax.fori_loop(0, count // group, turn, 0)
 
     def make_stiff(step):
         def body(e):
             at = brick * cells_x + e - HALO
             inside = jnp.where(jnp.logical_and(at >= 0, at < total_x), 1.0, 0.0).astype(F32)
             value = design[step, e]
-            stiff[e] = inside * (stiff_floor + (1.0 - stiff_floor) * (value * value * value))
+            stiff[e, rows_in] = inside * (stiff_floor + (1.0 - stiff_floor) * (value * value * value))
         return body
 
     def make_coef(step):
         def body(e):
-            s = stiff[e]
+            s = stiff[e, rows_in]
             free = (1 - support[e]).astype(F32)
-            sides = (stiff[e + 1], stiff[e - 1]) + inner_sides(s)
+            sides = (stiff[e + 1, rows_in], stiff[e - 1, rows_in],
+                     stiff[e, rows_next], stiff[e, rows_back]) + z_sides(s)
             faces = [0.5 * (s + side) for side in sides]
             total = faces[0]
             for face in faces[1:]:
                 total = total + face
             scale = free / (free * (total + mass_shift * s) + (1.0 - free))
-            outer = (None, None, y_last, y_first, z_last, z_first)
+            outer = (None, None, None, None, z_last, z_first)
             for j in range(6):
                 value = scale * faces[j]
                 coef[j, e] = value if outer[j] is None else jnp.where(outer[j], 0.0, value)
             here = design[step, e]
             for one in range(local_loads):
-                start = scale * (source[one, e] + weight_ref[one] * here)
+                force = source[one, e]
+                if step == 0:
+                    force = force + points[one, e]
+                    source[one, e] = force
+                start = scale * (force + weight_ref[one] * here)
                 resid[one, e] = start
-                direct[one, 0, e] = first_scale * start
+                direct[one][0][e, rows_in] = first_scale * start
         return body
 
     def make_sweep(k):
         keep, pull = factors[k]
 
         def body(e):
-            c = [coef[j, e] for j in range(6)]
-            for one in range(local_loads):
-                d = direct[one, k, e]
-                total = c[0] * direct[one, k, e + 1] + c[1] * direct[one, k, e - 1]
-                total = total + (c[2] * y_up(d) + c[3] * y_down(d))
-                total = total + (c[4] * z_up(d) + c[5] * z_down(d))
-                left = (resid[one, e] - d) + total
-                if k < SWEEPS - 2:
-                    resid[one, e] = left
-                    direct[one, k + 1, e] = keep * d + pull * left
-                else:
-                    full = keep * d + pull * left + d
-                    for older in range(k):
-                        full = full + direct[one, older, e]
-                    moved_x[one, e] = full
+            for part_rows in range(0, size_y, piece_rows):
+                inner = pl.ds(part_rows, piece_rows)
+                here, below, above = (pl.ds(PAD + part_rows + shift, piece_rows) for shift in (0, 1, -1))
+                c = [coef[j, e, inner] for j in range(6)]
+                for one in range(local_loads):
+                    level = direct[one][k]
+                    d = level[e, here]
+                    total = c[0] * level[e + 1, here] + c[1] * level[e - 1, here]
+                    total = total + (c[2] * level[e, below] + c[3] * level[e, above])
+                    total = total + (c[4] * z_up(d) + c[5] * z_down(d))
+                    left = (resid[one, e, inner] - d) + total
+                    if k < SWEEPS - 2:
+                        resid[one, e, inner] = left
+                        direct[one][k + 1][e, here] = keep * d + pull * left
+                    else:
+                        full = keep * d + pull * left + d
+                        for older in range(k):
+                            full = full + direct[one][older][e, here]
+                        moved_x[one, e, here] = full
         return body
 
     def make_sens(step):
         def body(e):
-            total = None
+            total = squares = up_gaps = None
             for one in range(local_loads):
-                f = moved_x[one, e]
+                f = moved_x[one, e, rows_in]
+                square = f * f
                 gaps = None
-                for beside in (moved_x[one, e + 1], moved_x[one, e - 1]) + inner_sides(f):
+                for beside in (moved_x[one, e + 1, rows_in], moved_x[one, e - 1, rows_in],
+                               moved_x[one, e, rows_next], moved_x[one, e, rows_back]):
                     gap = f - beside
                     gaps = gap * gap if gaps is None else gaps + gap * gap
-                value = mass_shift * (f * f) + 0.25 * gaps
+                gap = f - jnp.where(z_last, 0.0, z_up(f))
+                gap = gap * gap
+                value = mass_shift * square + 0.25 * (gaps + gap)
                 total = value if total is None else total + value
+                squares = square if squares is None else squares + square
+                up_gaps = gap if up_gaps is None else up_gaps + gap
+            total = total + 0.25 * jnp.where(z_first, squares, z_down(up_gaps))
             here = design[step, e]
-            sens[e] = (-3.0 * (1.0 - stiff_floor)) * (here * here) * total
+            sens[e, rows_in] = (-3.0 * (1.0 - stiff_floor)) * (here * here) * total
         return body
 
     edge_count = (
@@ -332,9 +396,10 @@
     def filter_layer(e):
         at = brick * cells_x + e - HALO
         end = jnp.where(jnp.logical_or(at == 0, at == total_x - 1), 1.0, 0.0).astype(F32)
-        value = sens[e]
-        total = 2.0 * value + sens[e + 1] + sens[e - 1]
-        for beside in inner_sides(value):
+        value = sens[e, rows_in]
+        total = 2.0 * value + sens[e + 1, rows_in] + sens[e - 1, rows_in]
+        total = total + sens[e, rows_next] + sens[e, rows_back]
+        for beside in z_sides(value):
             total = total + beside
         part[e - HALO] = total / (8.0 - (edge_count + end))
 
@@ -349,9 +414,10 @@
     for step in range(DESIGN_ITERS):
         final = step == DESIGN_ITERS - 1
         run(0, cells_x, make_stiff(step))
+        run(1, cells_x - 1, make_coef(step), 5)
         if step == 0:
-            run(0, cells_x, lambda e: add_points(e, 0))
-        run(1, cells_x - 1, make_coef(step))
+            pass_on(3)
+            rings_known()
         for k in range(SWEEPS - 1):
             run(2 + k, cells_x - 2 - k, make_sweep(k))
 
@@ -377,18 +443,20 @@
         for side in (0, 1):
             low_end = (lambda a, b: (a, b)) if side == 0 else (lambda a, b: (cells_x - b, cells_x - a))
             run(*low_end(-HALO, 0), make_stiff(step))
-            if step == 0:
-                run(*low_end(-WIDE, 0), lambda e: add_points(e, 0))
-            run(*low_end(-WIDE, 1), make_coef(step))
+            run(*low_end(-WIDE, 1), make_coef(step), 7)
         for side in (0, 1):
             low_end = (lambda a, b: (a, b)) if side == 0 else (lambda a, b: (cells_x - b, cells_x - a))
             for k in range(SWEEPS - 1):
-                run(*low_end(k + 1 - WIDE, 2 + k), make_sweep(k))
+                run(*low_end(k - WIDE, 2 + k), make_sweep(k))
         if final:
-            out_copy = pltpu.make_async_copy(moved_x.at[:, own], disp_ref, disp_sem)
+            out_copy = pltpu.make_async_copy(moved_x.at[:, own, rows_in], disp_ref, disp_sem)
             out_copy.start()
         run(-1, cells_x + 1, make_sens(step))
         run(0, cells_x, filter_layer)
+
+        if step == 0:
+            pl.semaphore_wait(column_in, XS - 1)
+            pl.semaphore_wait(partner_in, 1)
 
         to_pair = []
         for k in range(rows_hi):
@@ -422,34 +490,34 @@
             filt[:, my_slab] = total
 
         here = design[step, own, my_slab]
-        msg[step, 0] = jnp.concatenate(
-            [jnp.sum(jnp.abs(total), axis=0), jnp.sum(here, axis=0)], axis=0)
-        slots_one[step, me_one] = msg[step, 0]
-
-        def copy_one(k):
-            index = lax.rem(me_one + k, group_one)
-            return remote(msg.at[step, 0], slots_one.at[step, me_one], one_send.at[step, k],
-                          one_recv.at[step, me_one], member_one(index))
-
-        def came_one(k):
-            index = lax.rem(me_one + k, group_one)
-            return remote(msg.at[step, 0], slots_one.at[step, index], one_send.at[step, k],
-                          one_recv.at[step, index], member_one(index))
-
-        def copy_two(k):
-            index = lax.rem(me_two + k, group_two)
-            return remote(msg.at[step, 1], slots_two.at[step, me_two], two_send.at[step, k],
-                          two_recv.at[step, me_two], member_two(index))
-
-        def came_two(k):
-            index = lax.rem(me_two + k, group_two)
-            return remote(msg.at[step, 1], slots_two.at[step, index], two_send.at[step, k],
-                          two_recv.at[step, index], member_two(index))
-
-        def each(count, action):
-            lax.fori_loop(1, count, lambda k, c: (action(k), c)[1], 0)
-
-        each(group_one, lambda k: copy_one(k).start())
+
+        def fold(value):
+            value = jnp.sum(jnp.sum(value, axis=0), axis=0, keepdims=True)
+            return value + pltpu.roll(value, size_z // 2, 1)
+
+        left_half = lax.broadcasted_iota(jnp.int32, (1, size_z), 1) < size_z // 2
+        message = jnp.where(left_half, fold(jnp.abs(total)), fold(here))
+
+        def share(message, stage, slots, send, recv, me, count, member):
+            first_row = pl.ds(0, 1)
+            msg[step, stage, first_row] = message
+            slots[step, me, first_row] = message
+            for k in range(1, count):
+                remote(msg.at[step, stage, first_row], slots.at[step, me, first_row], send.at[step],
+                       recv.at[step], member(lax.rem(me + k, count))).start()
+
+            def finish():
+                ref = slots.at[step, pl.ds(0, count - 1), first_row]
+                remote(ref, ref, send.at[step], recv.at[step], partner).wait_recv()
+                return jnp.sum(slots[step, :, first_row], axis=0)
+
+            def drain():
+                ref = slots.at[step, pl.ds(0, count - 1), first_row]
+                remote(ref, ref, send.at[step], recv.at[step], partner).wait_send()
+
+            return finish, drain
+
+        finish_one, drain_one = share(message, 0, slots_one, one_send, one_recv, me_one, group_one, member_one)
 
         gathers = []
         if not final:
@@ -464,10 +532,7 @@
             copy.start()
             gathers.append(copy)
 
-        each(group_one, lambda k: came_one(k).wait_recv())
-        msg[step, 1] = jnp.sum(slots_one[step], axis=0)
-        slots_two[step, me_two] = msg[step, 1]
-        each(group_two, lambda k: copy_two(k).start())
+        finish_two, drain_two = share(finish_one(), 1, slots_two, two_send, two_recv, me_two, group_two, member_two)
 
         if not final:
             for k in order[:-1][::-1]:
@@ -482,10 +547,9 @@
                 ref = filt.at[:, slab_rows(index * CORES + 1 - core)]
                 remote(ref, ref, gatf_send.at[k], gatf_recv.at[k], partner).wait_recv()
 
-        each(group_two, lambda k: came_two(k).wait_recv())
-        sums = jnp.sum(slots_two[step], axis=0)
-        abs_total = jnp.sum(sums[0:slab], keepdims=True)
-        density_total = jnp.sum(sums[slab:2 * slab], keepdims=True)
+        sums = finish_two()
+        abs_total = jnp.sum(jnp.where(left_half, sums, 0.0), keepdims=True)
+        density_total = jnp.sum(jnp.where(left_half, 0.0, sums), keepdims=True)
         rate = step_size / (abs_total / total_cells + 1e-06)
         pull_down = volume_pull * (density_total / total_cells - volume_target)
 
@@ -511,8 +575,8 @@
 
         for copy in to_pair + to_row + gathers:
             copy.wait_send()
-        each(group_one, lambda k: copy_one(k).wait_send())
-        each(group_two, lambda k: copy_two(k).wait_send())
+        drain_one()
+        drain_two()
 
     for side, there in ((0, has_low), (1, has_high)):
         @pl.when(there)
@@ -539,13 +603,14 @@
     group_one, group_two = loads * YLS, zs * XS
     steps = DESIGN_ITERS
     layer = (size_y, size_z)
+    padded = (size_y + 2 * PAD, size_z)
     vmem = pltpu.VMEM
-    dma = pltpu.SemaphoreType.DMA
+    dma, regular = pltpu.SemaphoreType.DMA, pltpu.SemaphoreType.REGULAR
     space_any = pl.BlockSpec(memory_space=pl.ANY)
     space_vmem = pl.BlockSpec(memory_space=pltpu.VMEM)
     space_smem = pl.BlockSpec(memory_space=pltpu.SMEM)
     piece = (cells_x, slab, size_z)
-    return pl.pallas_call(
+    results = pl.pallas_call(
         functools.partial(kernel, dims),
         out_shape=(
             jax.ShapeDtypeStruct((cells_x, slab, size_z), F32),
@@ -559,21 +624,21 @@
             vmem((ext,) + layer, jnp.int32),
             vmem((cells_x,) + layer, jnp.int32),
             vmem((local_loads, ext) + layer, F32),
-            vmem((ext,) + layer, F32),
+            vmem((local_loads, ext) + layer, F32),
+            vmem((ext,) + padded, F32),
             vmem((6, ext) + layer, F32),
-            vmem((1,) + layer, F32),
-            vmem((local_loads, SWEEPS - 1, ext) + layer, F32),
+            ((vmem((ext,) + padded, F32),) * (SWEEPS - 1),) * local_loads,
             vmem((local_loads, ext) + layer, F32),
-            vmem((ext,) + layer, F32),
-            vmem((local_loads, ext) + layer, F32),
+            vmem((ext,) + padded, F32),
+            vmem((local_loads, ext) + padded, F32),
             vmem((cells_x,) + layer, F32),
             vmem((steps, rows_hi) + piece, F32),
             vmem((steps, rows_hi) + piece, F32),
             vmem((steps, rows_hi) + piece, F32),
             vmem((cells_x,) + layer, F32),
-            vmem((steps, 2, 2 * slab, size_z), F32),
-            vmem((steps, group_one, 2 * slab, size_z), F32),
-            vmem((steps, group_two, 2 * slab, size_z), F32),
+            vmem((steps, 2, 8, size_z), F32),
+            vmem((steps, group_one, 8, size_z), F32),
+            vmem((steps, group_two, 8, size_z), F32),
             dma((4,)),
             dma((2,)), dma((2,)),
             dma((2,)), dma((2,)), dma((2,)), dma((2,)),
@@ -581,12 +646,35 @@
             dma((steps, rows_hi)), dma((steps, rows_hi)),
             dma((steps, rows_hi)), dma((steps, rows_hi)),
             dma((rows_hi,)), dma((rows_hi,)), dma((rows_hi,)), dma((rows_hi,)),
-            dma((steps, group_one)), dma((steps, group_one)),
-            dma((steps, group_two)), dma((steps, group_two)),
+            dma((steps,)), dma((steps,)), dma((steps,)), dma((steps,)),
             dma,
+            regular((2, 2, max(YLS * rows_hi, zs) // 2)), regular, regular,
         ],
         compiler_params=pltpu.CompilerParams(collective_id=0, has_side_effects=True),
     )(density, passive, support, load_nodes, load_force, self_weight, body_force)
+    parts = [(0, slice(0, cells_x)), (1, slice(0, cells_x))]
+    parts += [(2, one) for one in range(local_loads)]
+    return pl.pallas_call(
+        functools.partial(hand_over, parts),
+        out_shape=tuple(jax.ShapeDtypeStruct(value.shape, value.dtype) for value in results),
+        in_specs=[space_any] * 3,
+        out_specs=(space_any,) * 3,
+        scratch_shapes=[vmem(value.shape, F32) for value in results]
+        + [dma((len(parts),)), dma((len(parts),))],
+    )(*results)
+
+
+def hand_over(parts, *refs):
+    sources, targets, held, (come, go) = refs[0:3], refs[3:6], refs[6:9], refs[9:]
+    into = [pltpu.make_async_copy(sources[i].at[at], held[i].at[at], come.at[n]) for n, (i, at) in enumerate(parts)]
+    out = [pltpu.make_async_copy(held[i].at[at], targets[i].at[at], go.at[n]) for n, (i, at) in enumerate(parts)]
+    for copy in into:
+        copy.start()
+    for first, second in zip(into, out):
+        first.wait()
+        second.start()
+    for copy in out:
+        copy.wait()
 
 
 def solution(mesh):

time: 122 us -> 90.5 us (0.74)
  Pallas kernels: 117 us -> 89.6 us
  local copies, waits for them, and re-layouts: 4.15 us -> 0 us
    pallas_call x1, Pallas kernels: 117 us -> 87.6 us  [body(): pl.pallas_call(functools.partial(kernel, dims), out_shape=(jax.ShapeDtype...]
    unnamed x5 -> x0, local copies, waits for them, and re-layouts: 4.15 us -> none
    pallas_call x0 -> x1, Pallas kernels: none -> 2 us  [body(): pl.pallas_call(functools.partial(hand_over, parts), out_shape=tuple((jax....]
where the time goes in v2:
time: 90.5 us; the launch traced here: 90.3 us
  Pallas kernels  89.6 us (99%)
    pallas_call x1, Pallas kernels, body(): pl.pallas_call(functools.partial(kernel, dims), out_shape=(jax.ShapeDtype...  87.6 us
    pallas_call x1, Pallas kernels, body(): pl.pallas_call(functools.partial(hand_over, parts), out_shape=tuple((jax....  2 us

profile of v2, /device:TPU:1, one launch (start us, length us, event | category | flops | bytes accessed | tf_op | source)
XLA Modules:
  0.0 90.3 jit_solution(7369602736644345270)
XLA Ops:
  0.6 87.6 %shard_map.94 = (f32[12,8,128]{2,1,0:T(8,128)}, f32[12,8,128]{2,1,0:T(8,128)}, f32[2,12,64,128]{3,2,1,0:T(8,128)}) custom-call(f32[12,64,128]{2,1,0:T(8,128)} %density_ref.1, s32[12,64,128]{2,1,0:T(8,128)} %passive_ref.1, s32[12,64,128]{2,1,0:T(8,128)} %support_ref.1, s32[2,64]{1,0:T(2,128)} %nodes_ref.1, f32[2,64]{1,0:T(2,128)} %force_ref.1, f32[2]{0:T(128)} %weight_ref.1, ...), custom_call_target="tpu_custom_call" | custom-call | tf_op jit(solution)/shard_map/pallas_call | solution.py:613
  88.3 2.0 %shard_map.95 = (f32[12,8,128]{2,1,0:T(8,128)}, f32[12,8,128]{2,1,0:T(8,128)}, f32[2,12,64,128]{3,2,1,0:T(8,128)}) custom-call(f32[12,8,128]{2,1,0:T(8,128)} %get-tuple-element.6.refs_0_, f32[12,8,128]{2,1,0:T(8,128)} %get-tuple-element.7.refs_1_, f32[2,12,64,128]{3,2,1,0:T(8,128)} %get-tuple-element.8.refs_2_), custom_call_target="tpu_custom_call" | custom-call | tf_op jit(solution)/shard_map/pallas_call | solution.py:657

commit v3 on v2

--- a/solution.py
+++ b/solution.py
@@ -54,6 +54,7 @@
     load_sems, body_send, body_recv, sup_send, sup_recv, supf_send, supf_recv,
     des_send, des_recv, desf_send, desf_recv,
     pair_send, pair_recv, row_send, row_recv, gath_send, gath_recv, gatf_send, gatf_recv,
+    pas_send, pas_recv, pasf_send, pasf_recv, fil_send, fil_recv, filf_send, filf_recv,
     one_send, one_recv, two_send, two_recv, disp_sem, hello, column_in, partner_in,
 ):
     loads, bricks, cells_x, size_y, size_z, nodes = dims
@@ -104,7 +105,7 @@
     own = pl.ds(HALO, cells_x)
     loads_in = [
         pltpu.make_async_copy(density_ref, design.at[0, own], load_sems.at[0]),
-        pltpu.make_async_copy(passive_ref, passive, load_sems.at[1]),
+        pltpu.make_async_copy(passive_ref, passive.at[own], load_sems.at[1]),
         pltpu.make_async_copy(support_ref, support.at[own], load_sems.at[2]),
         pltpu.make_async_copy(body_ref, source.at[:, own], load_sems.at[3]),
     ]
@@ -195,16 +196,10 @@
     loads_in[1].wait()
 
     def first_design(layer, carry):
-        design[0, layer + HALO] = passive_apply(design[0, layer + HALO], passive[layer])
+        design[0, layer + HALO] = passive_apply(design[0, layer + HALO], passive[layer + HALO])
         return carry
 
     lax.fori_loop(0, cells_x, first_design, 0)
-
-    def send_design(step):
-        copies = halo_copies(design, HALO, design, HALO, des_send.at[step], des_recv.at[step],
-                             (step,), (mine, slice(None)))
-        start_halo(copies)
-        return copies
 
     def clear(first):
         zero = jnp.zeros((size_y, size_z), F32)
@@ -223,8 +218,12 @@
     def _():
         clear(last)
 
-    design_copies = [send_design(0)]
+    half_rows = (mine, slice(None))
+    des_copies = halo_copies(design, HALO, design, HALO, des_send, des_recv, (0,), half_rows)
+    start_halo(des_copies)
     start_halo(body_copies)
+    pas_copies = halo_copies(passive_ref, 0, passive, HALO, pas_send, pas_recv, (), half_rows)
+    start_halo(pas_copies)
     pass_on(0)
 
     blank = jnp.zeros((PAD, size_z), F32)
@@ -411,43 +410,79 @@
 
     my_slab = slab_rows(load)
 
+    both_sides = ((0, has_low), (1, has_high))
+
+    def to_partner(ref, lead, width, side, send, recv, rows):
+        first = HALO - width if side == 0 else last
+        ref = ref.at[lead + (pl.ds(first, width), rows)]
+        return remote(ref, ref, send, recv, partner)
+
+    def pass_to_partner(ref, lead, width, side, near, far):
+        landed(ref, width, near[1], near[0], lead, half_rows, side).wait_recv()
+        to_partner(ref, lead, width, side, far[0].at[side], far[1].at[side], mine).start()
+
+    sup_sems, des_sems, pas_sems = (
+        ((sup_send, sup_recv), (supf_send, supf_recv)),
+        ((des_send, des_recv), (desf_send, desf_recv)),
+        ((pas_send, pas_recv), (pasf_send, pasf_recv)),
+    )
+    halo_kinds = ((support, (), WIDE, sup_sems), (design, (0,), HALO, des_sems), (passive, (), HALO, pas_sems))
+
+    def came_from_partner(kind, side):
+        ref, lead, width, sems = kind
+        to_partner(ref, lead, width, side, sems[1][0].at[side], sems[1][1].at[side], others).wait_recv()
+
+    def pass_filtered(k):
+        rows = slab_rows(lax.rem(row + rows_hi - k, rows_hi) * CORES + core)
+        down = remote(filt.at[pl.ds(HALO, HALO), rows], filt.at[pl.ds(last, HALO), rows],
+                      fil_send.at[k, 0], fil_recv.at[k, 1], low)
+        up = remote(filt.at[pl.ds(cells_x, HALO), rows], filt.at[pl.ds(0, HALO), rows],
+                    fil_send.at[k, 1], fil_recv.at[k, 0], high)
+        return down, up
+
+    def filtered_halo(k, side, whose):
+        index = lax.rem(row + rows_hi - k, rows_hi) * CORES + whose
+        return filt.at[pl.ds(0 if side == 0 else last, HALO), slab_rows(index)]
+
     for step in range(DESIGN_ITERS):
         final = step == DESIGN_ITERS - 1
-        run(0, cells_x, make_stiff(step))
-        run(1, cells_x - 1, make_coef(step), 5)
         if step == 0:
+            run(0, cells_x, make_stiff(step))
+            run(1, cells_x - 1, make_coef(step), 5)
             pass_on(3)
             rings_known()
-        for k in range(SWEEPS - 1):
-            run(2 + k, cells_x - 2 - k, make_sweep(k))
-
-        for side, there in ((0, has_low), (1, has_high)):
-            first = HALO - WIDE if side == 0 else last
-
-            @pl.when(there)
-            def _(side=side, there=there, first=first, step=step):
-                if step == 0:
-                    landed(support, WIDE, sup_recv, sup_send, (), (mine, slice(None)), side).wait_recv()
-                    ref = support.at[pl.ds(first, WIDE), mine]
-                    remote(ref, ref, supf_send.at[side], supf_recv.at[side], partner).start()
-                landed(design, HALO, des_recv.at[step], des_send.at[step], (step,), (mine, slice(None)), side).wait_recv()
-                ref = design.at[step, pl.ds(0 if side == 0 else last, HALO), mine]
-                remote(ref, ref, desf_send.at[step, side], desf_recv.at[step, side], partner).start()
-                if step == 0:
+            for k in range(SWEEPS - 1):
+                run(2 + k, cells_x - 2 - k, make_sweep(k))
+
+            for side, there in both_sides:
+                @pl.when(there)
+                def _(side=side):
+                    for ref, lead, width, (near, far) in halo_kinds[:2]:
+                        pass_to_partner(ref, lead, width, side, near, far)
+
+            for side, there in both_sides:
+                @pl.when(there)
+                def _(side=side):
                     landed(source, WIDE, body_recv, body_send, (slice(None),), body_rows, side).wait_recv()
-                    ref = support.at[pl.ds(first, WIDE), others]
-                    remote(ref, ref, supf_send.at[side], supf_recv.at[side], partner).wait_recv()
-                ref = design.at[step, pl.ds(0 if side == 0 else last, HALO), others]
-                remote(ref, ref, desf_send.at[step, side], desf_recv.at[step, side], partner).wait_recv()
-
-        for side in (0, 1):
-            low_end = (lambda a, b: (a, b)) if side == 0 else (lambda a, b: (cells_x - b, cells_x - a))
-            run(*low_end(-HALO, 0), make_stiff(step))
-            run(*low_end(-WIDE, 1), make_coef(step), 7)
-        for side in (0, 1):
-            low_end = (lambda a, b: (a, b)) if side == 0 else (lambda a, b: (cells_x - b, cells_x - a))
+                    for kind in halo_kinds[:2]:
+                        came_from_partner(kind, side)
+
+                low_end = (lambda a, b: (a, b)) if side == 0 else (lambda a, b: (cells_x - b, cells_x - a))
+                run(*low_end(-HALO, 0), make_stiff(step))
+                run(*low_end(-WIDE, 1), make_coef(step), 7)
+                for k in range(SWEEPS - 1):
+                    run(*low_end(k + 1 - WIDE, 2 + k), make_sweep(k), 7)
+
+            for side, there in both_sides:
+                @pl.when(there)
+                def _(side=side):
+                    ref, lead, width, (near, far) = halo_kinds[2]
+                    pass_to_partner(ref, lead, width, side, near, far)
+        else:
+            run(-HALO, cells_x + HALO, make_stiff(step))
+            run(-WIDE, cells_x + WIDE, make_coef(step))
             for k in range(SWEEPS - 1):
-                run(*low_end(k - WIDE, 2 + k), make_sweep(k))
+                run(k + 1 - WIDE, cells_x + WIDE - 1 - k, make_sweep(k), 5)
         if final:
             out_copy = pltpu.make_async_copy(moved_x.at[:, own, rows_in], disp_ref, disp_sem)
             out_copy.start()
@@ -484,10 +519,10 @@
             copy.wait_recv()
             total = total + row_in[step, k]
         if final:
-            total = moment_decay * filt[:, my_slab] + total
+            total = moment_decay * filt[own, my_slab] + total
             moment_ref[...] = total
         else:
-            filt[:, my_slab] = total
+            filt[own, my_slab] = total
 
         here = design[step, own, my_slab]
 
@@ -523,11 +558,12 @@
         if not final:
             for k in order[:-1]:
                 index = other_row(k)
-                copy = remote(filt.at[:, my_slab], filt.at[:, my_slab], gath_send.at[k],
+                copy = remote(filt.at[own, my_slab], filt.at[own, my_slab], gath_send.at[k],
                               gath_recv.at[k], device(index * CORES + core, brick))
                 copy.start()
                 gathers.append(copy)
-            copy = remote(filt.at[:, my_slab], filt.at[:, my_slab], gatf_send.at[0],
+            start_halo(pass_filtered(0))
+            copy = remote(filt.at[own, my_slab], filt.at[own, my_slab], gatf_send.at[0],
                           gatf_recv.at[0], partner)
             copy.start()
             gathers.append(copy)
@@ -537,15 +573,33 @@
         if not final:
             for k in order[:-1][::-1]:
                 index = lax.rem(row + rows_hi - k, rows_hi)
-                ref = filt.at[:, slab_rows(index * CORES + core)]
+                ref = filt.at[own, slab_rows(index * CORES + core)]
                 remote(ref, ref, gath_send.at[k], gath_recv.at[k], partner).wait_recv()
+                start_halo(pass_filtered(k))
                 copy = remote(ref, ref, gatf_send.at[k], gatf_recv.at[k], partner)
                 copy.start()
                 gathers.append(copy)
-            for k in [0] + order[:-1][::-1]:
+            came_in = [0] + order[:-1][::-1]
+            for k in came_in:
+                for side, there in both_sides:
+                    @pl.when(there)
+                    def _(k=k, side=side):
+                        ref = filtered_halo(k, side, core)
+                        remote(ref, ref, fil_send.at[k, side], fil_recv.at[k, side], partner).wait_recv()
+                        remote(ref, ref, filf_send.at[k, side], filf_recv.at[k, side], partner).start()
+            for k in came_in:
                 index = lax.rem(row + rows_hi - k, rows_hi)
-                ref = filt.at[:, slab_rows(index * CORES + 1 - core)]
+                ref = filt.at[own, slab_rows(index * CORES + 1 - core)]
                 remote(ref, ref, gatf_send.at[k], gatf_recv.at[k], partner).wait_recv()
+                for side, there in both_sides:
+                    @pl.when(there)
+                    def _(k=k, side=side):
+                        ref = filtered_halo(k, side, 1 - core)
+                        remote(ref, ref, filf_send.at[k, side], filf_recv.at[k, side], partner).wait_recv()
+            for side, there in both_sides:
+                @pl.when(there)
+                def _(side=side):
+                    came_from_partner(halo_kinds[2], side)
 
         sums = finish_two()
         abs_total = jnp.sum(jnp.where(left_half, sums, 0.0), keepdims=True)
@@ -560,36 +614,40 @@
         if final:
             def last_design(layer, carry):
                 new_ref[layer] = updated(design[step, layer + HALO, my_slab],
-                                         moment_ref[layer], passive[layer, my_slab])
+                                         moment_ref[layer], passive[layer + HALO, my_slab])
                 return carry
 
             lax.fori_loop(0, cells_x, last_design, 0)
         else:
-            def next_design(layer, carry):
-                design[step + 1, layer + HALO] = updated(
-                    design[step, layer + HALO], filt[layer], passive[layer])
-                return carry
-
-            lax.fori_loop(0, cells_x, next_design, 0)
-            design_copies.append(send_design(step + 1))
+            def next_design(e):
+                design[step + 1, e] = updated(design[step, e], filt[e], passive[e])
+
+            @pl.when(has_low)
+            def _():
+                run(-HALO, 0, next_design, 7)
+
+            run(0, cells_x, next_design, 6)
+
+            @pl.when(has_high)
+            def _():
+                run(cells_x, cells_x + HALO, next_design, 7)
 
         for copy in to_pair + to_row + gathers:
             copy.wait_send()
         drain_one()
         drain_two()
 
-    for side, there in ((0, has_low), (1, has_high)):
+    for side, there in both_sides:
         @pl.when(there)
         def _(side=side):
-            body_copies[side].wait_send()
-            sup_copies[side].wait_send()
-            first = HALO - WIDE if side == 0 else last
-            ref = support.at[pl.ds(first, WIDE), mine]
-            remote(ref, ref, supf_send.at[side], supf_recv.at[side], partner).wait_send()
-            for step in range(DESIGN_ITERS):
-                design_copies[step][side].wait_send()
-                ref = design.at[step, pl.ds(0 if side == 0 else last, HALO), mine]
-                remote(ref, ref, desf_send.at[step, side], desf_recv.at[step, side], partner).wait_send()
+            for copies in (body_copies, sup_copies, des_copies, pas_copies):
+                copies[side].wait_send()
+            for ref, lead, width, sems in halo_kinds:
+                to_partner(ref, lead, width, side, sems[1][0].at[side], sems[1][1].at[side], mine).wait_send()
+            for k in range(rows_hi):
+                pass_filtered(k)[side].wait_send()
+                ref = filtered_halo(k, side, core)
+                remote(ref, ref, filf_send.at[k, side], filf_recv.at[k, side], partner).wait_send()
     out_copy.wait()
 
 
@@ -622,7 +680,7 @@
         scratch_shapes=[
             vmem((steps, ext) + layer, F32),
             vmem((ext,) + layer, jnp.int32),
-            vmem((cells_x,) + layer, jnp.int32),
+            vmem((ext,) + layer, jnp.int32),
             vmem((local_loads, ext) + layer, F32),
             vmem((local_loads, ext) + layer, F32),
             vmem((ext,) + padded, F32),
@@ -635,17 +693,19 @@
             vmem((steps, rows_hi) + piece, F32),
             vmem((steps, rows_hi) + piece, F32),
             vmem((steps, rows_hi) + piece, F32),
-            vmem((cells_x,) + layer, F32),
+            vmem((ext,) + layer, F32),
             vmem((steps, 2, 8, size_z), F32),
             vmem((steps, group_one, 8, size_z), F32),
             vmem((steps, group_two, 8, size_z), F32),
             dma((4,)),
             dma((2,)), dma((2,)),
             dma((2,)), dma((2,)), dma((2,)), dma((2,)),
-            dma((steps, 2)), dma((steps, 2)), dma((steps, 2)), dma((steps, 2)),
+            dma((2,)), dma((2,)), dma((2,)), dma((2,)),
             dma((steps, rows_hi)), dma((steps, rows_hi)),
             dma((steps, rows_hi)), dma((steps, rows_hi)),
             dma((rows_hi,)), dma((rows_hi,)), dma((rows_hi,)), dma((rows_hi,)),
+            dma((2,)), dma((2,)), dma((2,)), dma((2,)),
+            dma((rows_hi, 2)), dma((rows_hi, 2)), dma((rows_hi, 2)), dma((rows_hi, 2)),
             dma((steps,)), dma((steps,)), dma((steps,)), dma((steps,)),
             dma,
             regular((2, 2, max(YLS * rows_hi, zs) // 2)), regular, regular,

time: 90.5 us -> 87 us (0.961)
  Pallas kernels: 89.6 us -> 86.2 us
    pallas_call x1, Pallas kernels: 87.6 us -> 84.2 us  [body(): pl.pallas_call(functools.partial(kernel, dims), out_shape=(jax.ShapeDtype...]
where the time goes in v3:
time: 87 us; the launch traced here: 86.8 us
  Pallas kernels  86.2 us (99%)
    pallas_call x1, Pallas kernels, body(): pl.pallas_call(functools.partial(kernel, dims), out_shape=(jax.ShapeDtype...  84.2 us
    pallas_call x1, Pallas kernels, body(): pl.pallas_call(functools.partial(hand_over, parts), out_shape=tuple((jax....  2 us

profile of v3, /device:TPU:1, one launch (start us, length us, event | category | flops | bytes accessed | tf_op | source)
XLA Modules:
  0.0 86.8 jit_solution(15588006873531810648)
XLA Ops:
  0.6 84.2 %shard_map.94 = (f32[12,8,128]{2,1,0:T(8,128)}, f32[12,8,128]{2,1,0:T(8,128)}, f32[2,12,64,128]{3,2,1,0:T(8,128)}) custom-call(f32[12,64,128]{2,1,0:T(8,128)} %density_ref.1, s32[12,64,128]{2,1,0:T(8,128)} %passive_ref.1, s32[12,64,128]{2,1,0:T(8,128)} %support_ref.1, s32[2,64]{1,0:T(2,128)} %nodes_ref.1, f32[2,64]{1,0:T(2,128)} %force_ref.1, f32[2]{0:T(128)} %weight_ref.1, ...), custom_call_target="tpu_custom_call" | custom-call | tf_op jit(solution)/shard_map/pallas_call | solution.py:671
  84.8 2.0 %shard_map.95 = (f32[12,8,128]{2,1,0:T(8,128)}, f32[12,8,128]{2,1,0:T(8,128)}, f32[2,12,64,128]{3,2,1,0:T(8,128)}) custom-call(f32[12,8,128]{2,1,0:T(8,128)} %get-tuple-element.6.refs_0_, f32[12,8,128]{2,1,0:T(8,128)} %get-tuple-element.7.refs_1_, f32[2,12,64,128]{3,2,1,0:T(8,128)} %get-tuple-element.8.refs_2_), custom_call_target="tpu_custom_call" | custom-call | tf_op jit(solution)/shard_map/pallas_call | solution.py:717

commit v4 on v3

--- a/solution.py
+++ b/solution.py
@@ -188,9 +188,13 @@
         return remote(ref, ref, send.at[side], recv.at[side], partner)
 
     body_rows = (slice(None), slice(None))
-    body_copies = halo_copies(body_ref, 0, source, WIDE, body_send, body_recv, (slice(None),), body_rows)
+    body_copies = [
+        halo_copies(body_ref, 0, source, WIDE, body_send.at[one], body_recv.at[one], (one,), body_rows)
+        for one in range(local_loads)
+    ]
     sup_copies = halo_copies(support_ref, 0, support, WIDE, sup_send, sup_recv, (), (mine, slice(None)))
     start_halo(sup_copies)
+    start_halo(body_copies[0])
 
     loads_in[0].wait()
     loads_in[1].wait()
@@ -221,7 +225,8 @@
     half_rows = (mine, slice(None))
     des_copies = halo_copies(design, HALO, design, HALO, des_send, des_recv, (0,), half_rows)
     start_halo(des_copies)
-    start_halo(body_copies)
+    for copies in body_copies[1:]:
+        start_halo(copies)
     pas_copies = halo_copies(passive_ref, 0, passive, HALO, pas_send, pas_recv, (), half_rows)
     start_halo(pas_copies)
     pass_on(0)
@@ -444,6 +449,36 @@
         index = lax.rem(row + rows_hi - k, rows_hi) * CORES + whose
         return filt.at[pl.ds(0 if side == 0 else last, HALO), slab_rows(index)]
 
+    cut = (cells_x - 2) // 2
+    pieces = (pl.ds(0, cut), pl.ds(cut, cells_x - cut))
+    order = sorted(range(1, rows_hi), key=lambda k: -min(k, rows_hi - k)) + [0]
+    to_pair = [[] for _ in range(DESIGN_ITERS)]
+    to_row = [[] for _ in range(DESIGN_ITERS)]
+
+    def pair_copy(step, piece, k, rows):
+        at, index = pieces[piece], other_row(k)
+        return remote(part.at[at, rows], pair_in.at[step, index, at], pair_send.at[step, piece, k],
+                      pair_recv.at[step, piece, index], partner)
+
+    def pair_piece(step, piece):
+        for k in order:
+            copy = pair_copy(step, piece, k, slab_rows(other_row(k) * CORES + 1 - core))
+            copy.start()
+            to_pair[step].append(copy)
+
+    def row_piece(step, piece):
+        at = pieces[piece]
+        for k in order:
+            index = other_row(k)
+            rows = slab_rows(index * CORES + core)
+            pair_copy(step, piece, k, rows).wait_recv()
+            pair_out[step, k, at] = part[at, rows] + pair_in[step, index, at]
+            if k:
+                copy = remote(pair_out.at[step, k, at], row_in.at[step, k, at], row_send.at[step, piece, k],
+                              row_recv.at[step, piece, k], device(index * CORES + core, brick))
+                copy.start()
+                to_row[step].append(copy)
+
     for step in range(DESIGN_ITERS):
         final = step == DESIGN_ITERS - 1
         if step == 0:
@@ -463,15 +498,24 @@
             for side, there in both_sides:
                 @pl.when(there)
                 def _(side=side):
-                    landed(source, WIDE, body_recv, body_send, (slice(None),), body_rows, side).wait_recv()
+                    for one in range(local_loads):
+                        landed(source, WIDE, body_recv.at[one], body_send.at[one], (one,), body_rows, side).wait_recv()
                     for kind in halo_kinds[:2]:
                         came_from_partner(kind, side)
 
                 low_end = (lambda a, b: (a, b)) if side == 0 else (lambda a, b: (cells_x - b, cells_x - a))
                 run(*low_end(-HALO, 0), make_stiff(step))
                 run(*low_end(-WIDE, 1), make_coef(step), 7)
+                if side == 1:
+                    pl.semaphore_wait(column_in, XS - 1)
+                    pl.semaphore_wait(partner_in, 1)
+                    row_piece(step, 0)
                 for k in range(SWEEPS - 1):
                     run(*low_end(k + 1 - WIDE, 2 + k), make_sweep(k), 7)
+                if side == 0:
+                    run(-1, cut + 1, make_sens(step), 7)
+                    run(0, cut, filter_layer, 7)
+                    pair_piece(step, 0)
 
             for side, there in both_sides:
                 @pl.when(there)
@@ -486,37 +530,20 @@
         if final:
             out_copy = pltpu.make_async_copy(moved_x.at[:, own, rows_in], disp_ref, disp_sem)
             out_copy.start()
-        run(-1, cells_x + 1, make_sens(step))
-        run(0, cells_x, filter_layer)
-
-        if step == 0:
-            pl.semaphore_wait(column_in, XS - 1)
-            pl.semaphore_wait(partner_in, 1)
-
-        to_pair = []
-        for k in range(rows_hi):
-            index = other_row(k)
-            rows = slab_rows(index * CORES + 1 - core)
-            copy = remote(part.at[:, rows], pair_in.at[step, index], pair_send.at[step, k],
-                          pair_recv.at[step, index], partner)
-            copy.start()
-            to_pair.append(copy)
-        to_row = []
-        order = sorted(range(1, rows_hi), key=lambda k: -min(k, rows_hi - k)) + [0]
-        for k in order:
-            index = other_row(k)
-            rows = slab_rows(index * CORES + core)
-            remote(part.at[:, rows], pair_in.at[step, index], pair_send.at[step, k],
-                   pair_recv.at[step, index], partner).wait_recv()
-            pair_out[step, k] = part[:, rows] + pair_in[step, index]
-            if k:
-                copy = remote(pair_out.at[step, k], row_in.at[step, k], row_send.at[step, k],
-                              row_recv.at[step, k], device(index * CORES + core, brick))
-                copy.start()
-                to_row.append(copy)
+        if step:
+            run(-1, cut + 1, make_sens(step), 7)
+            run(0, cut, filter_layer, 7)
+            pair_piece(step, 0)
+        run(cut + 1, cells_x + 1, make_sens(step), 7)
+        if step:
+            row_piece(step, 0)
+        run(cut, cells_x, filter_layer, 7)
+        pair_piece(step, 1)
+        row_piece(step, 1)
         total = pair_out[step, 0]
-        for copy, k in zip(to_row, order):
+        for copy in to_row[step]:
             copy.wait_recv()
+        for k in order[:-1]:
             total = total + row_in[step, k]
         if final:
             total = moment_decay * filt[own, my_slab] + total
@@ -632,7 +659,7 @@
             def _():
                 run(cells_x, cells_x + HALO, next_design, 7)
 
-        for copy in to_pair + to_row + gathers:
+        for copy in to_pair[step] + to_row[step] + gathers:
             copy.wait_send()
         drain_one()
         drain_two()
@@ -640,7 +667,7 @@
     for side, there in both_sides:
         @pl.when(there)
         def _(side=side):
-            for copies in (body_copies, sup_copies, des_copies, pas_copies):
+            for copies in body_copies + [sup_copies, des_copies, pas_copies]:
                 copies[side].wait_send()
             for ref, lead, width, sems in halo_kinds:
                 to_partner(ref, lead, width, side, sems[1][0].at[side], sems[1][1].at[side], mine).wait_send()
@@ -698,11 +725,11 @@
             vmem((steps, group_one, 8, size_z), F32),
             vmem((steps, group_two, 8, size_z), F32),
             dma((4,)),
-            dma((2,)), dma((2,)),
+            dma((local_loads, 2)), dma((local_loads, 2)),
             dma((2,)), dma((2,)), dma((2,)), dma((2,)),
             dma((2,)), dma((2,)), dma((2,)), dma((2,)),
-            dma((steps, rows_hi)), dma((steps, rows_hi)),
-            dma((steps, rows_hi)), dma((steps, rows_hi)),
+            dma((steps, 2, rows_hi)), dma((steps, 2, rows_hi)),
+            dma((steps, 2, rows_hi)), dma((steps, 2, rows_hi)),
             dma((rows_hi,)), dma((rows_hi,)), dma((rows_hi,)), dma((rows_hi,)),
             dma((2,)), dma((2,)), dma((2,)), dma((2,)),
             dma((rows_hi, 2)), dma((rows_hi, 2)), dma((rows_hi, 2)), dma((rows_hi, 2)),

time: 87 us -> 85.5 us (0.983)
  Pallas kernels: 86.2 us -> 84.7 us
    pallas_call x1, Pallas kernels: 84.2 us -> 82.7 us  [body(): pl.pallas_call(functools.partial(kernel, dims), out_shape=(jax.ShapeDtype...]
where the time goes in v4:
time: 85.5 us; the launch traced here: 85.4 us
  Pallas kernels  84.7 us (99%)
    pallas_call x1, Pallas kernels, body(): pl.pallas_call(functools.partial(kernel, dims), out_shape=(jax.ShapeDtype...  82.7 us
    pallas_call x1, Pallas kernels, body(): pl.pallas_call(functools.partial(hand_over, parts), out_shape=tuple((jax....  2 us

profile of v4, /device:TPU:1, one launch (start us, length us, event | category | flops | bytes accessed | tf_op | source)
XLA Modules:
  0.0 85.4 jit_solution(15166514940216723121)
XLA Ops:
  0.6 82.7 %shard_map.94 = (f32[12,8,128]{2,1,0:T(8,128)}, f32[12,8,128]{2,1,0:T(8,128)}, f32[2,12,64,128]{3,2,1,0:T(8,128)}) custom-call(f32[12,64,128]{2,1,0:T(8,128)} %density_ref.1, s32[12,64,128]{2,1,0:T(8,128)} %passive_ref.1, s32[12,64,128]{2,1,0:T(8,128)} %support_ref.1, s32[2,64]{1,0:T(2,128)} %nodes_ref.1, f32[2,64]{1,0:T(2,128)} %force_ref.1, f32[2]{0:T(128)} %weight_ref.1, ...), custom_call_target="tpu_custom_call" | custom-call | tf_op jit(solution)/shard_map/pallas_call | solution.py:698
  83.4 2.0 %shard_map.95 = (f32[12,8,128]{2,1,0:T(8,128)}, f32[12,8,128]{2,1,0:T(8,128)}, f32[2,12,64,128]{3,2,1,0:T(8,128)}) custom-call(f32[12,8,128]{2,1,0:T(8,128)} %get-tuple-element.6.refs_0_, f32[12,8,128]{2,1,0:T(8,128)} %get-tuple-element.7.refs_1_, f32[2,12,64,128]{3,2,1,0:T(8,128)} %get-tuple-element.8.refs_2_), custom_call_target="tpu_custom_call" | custom-call | tf_op jit(solution)/shard_map/pallas_call | solution.py:744
